TPU v7x, 128 devices: a whole 4x4x4 slice. The times are simulated.
128 devices in a mesh: col: 32 (over x, y, core), row: 4 (over z).
Axes of the slice: x: 4, y: 4, z: 4, core: 2. Of those that a mesh axis runs over, the one named last changes fastest.
Arguments:
- targets: float32 [4, 32, 1024, 128], P(None, 'col', 'row'), as said below
- src_panels: bfloat16 [2048, 1024, 128], P('col', 'row')
- live_counts: int32 [32], P('col'), may hold values from 1 to 64, 1024 in all
- dest_owner: int32 [2048, 4], P('col'), may hold values from 0 to 31
- relative_map: int32 [2048, 4, 8], P('col', None, 'row'), may hold values from 0 to 1, as said below
- diag_row: int32 [4, 32], replicated, may hold values from 0 to 3
- parent: int32 [3, 32], replicated, may hold values from 0 to 31
- chain_map: int32 [3, 32, 8], P(None, None, 'row'), may hold values from 0 to 1, as said below
Outputs:
- factors: float32 [4, 32, 1024, 128], P(None, 'col', 'row')
Inputs may be any that keep to these rules, and one draw needn't show every extreme that they name: For each i, s and row group r, the 2 entries relative_map[i, s, r * 2 : (r + 1) * 2] are a permutation of 0 to 1; on r = diag_row[s, dest_owner[i, s]] it maps 0 to 0. For each s, k and row group r, the 2 entries chain_map[s, k, r * 2 : (r + 1) * 2] are a permutation of 0 to 1; on r = diag_row[s + 1, parent[s, k]] it maps 1 to 0. `live_counts`: the counts sum to 1024 and the largest is 64. `targets`: every diagonal block after all updates is symmetric positive definite.
All inputs are finite; a program needn't handle non-finite values. No bound on the sum of `live_counts` on one device may be relied on, other than what follows from the above.
Results may differ from a plain program's by a relative error of at most 0.0003.
Values may be sent and summed in bfloat16 or wider, within the bound.
A program may use at most 128 MiB of HBM per device.

v0:
```python
import jax
import jax.numpy as jnp
from jax import lax
from jax.sharding import PartitionSpec as P


def spread(block, axis, owner):
    block = jnp.where(lax.axis_index(axis) == owner, block, jnp.zeros_like(block))
    return lax.psum(block, axis)


def lower_solve(lower_block, blocks):
    return lax.linalg.triangular_solve(
        jnp.broadcast_to(lower_block, blocks.shape),
        blocks,
        left_side=False,
        lower=True,
        transpose_a=True,
    )


def local(targets, src_panels, live_counts, dest_owner, relative_map, diag_row, parent, chain_map):
    col_count = lax.axis_size("col")
    owner_index = lax.axis_index("col")
    row_index = lax.axis_index("row")
    src_count = src_panels.shape[0]
    block_width = src_panels.shape[2]
    local_blocks = src_panels.shape[1] // block_width
    sections = targets.shape[0]
    panels = src_panels.reshape(src_count, local_blocks, block_width, block_width)
    alive_mask = (jnp.arange(src_count) < live_counts[0]).astype(jnp.float32)
    column_heads = lax.all_gather(panels[:, 0][None], "row", axis=0, tiled=True)
    source_root = diag_row[jnp.arange(sections)[None, :], dest_owner]
    block_index = jnp.arange(local_blocks)
    sources = jnp.arange(src_count)
    results = []
    for s in range(sections):
        columns = column_heads[source_root[:, s], sources]
        source_products = jnp.einsum(
            "iqab,icb->iqac", panels, columns, preferred_element_type=jnp.float32
        )
        source_products = source_products * alive_mask[:, None, None, None]
        source_slot_ids = dest_owner[:, s, None] * local_blocks + relative_map[:, s, :]
        slot_sums = jax.ops.segment_sum(
            source_products.reshape(src_count * local_blocks, block_width, block_width),
            source_slot_ids.reshape(-1),
            num_segments=col_count * local_blocks,
        )
        if s > 0:
            child_rows = results[-1].astype(jnp.bfloat16)
            parent_root = diag_row[s, parent[s - 1, owner_index]]
            column = spread(child_rows[block_width : 2 * block_width], "row", parent_root)
            products = jnp.einsum(
                "qab,cb->qac",
                child_rows.reshape(local_blocks, block_width, block_width),
                column,
                preferred_element_type=jnp.float32,
            )
            kept_mask = jnp.logical_not(
                (diag_row[s - 1, owner_index] == row_index) & (block_index == 0)
            )
            products = products * kept_mask[:, None, None].astype(jnp.float32)
            slot_ids = parent[s - 1, owner_index] * local_blocks + chain_map[s - 1, owner_index]
            slot_sums = slot_sums.at[slot_ids].add(products)
        gathered = lax.psum_scatter(
            slot_sums.reshape(col_count * local_blocks * block_width, block_width),
            "col",
            scatter_dimension=0,
            tiled=True,
        )
        updated = targets[s, 0] - gathered
        root_row = diag_row[s, owner_index]
        is_root = row_index == root_row
        blocks = updated.reshape(local_blocks, block_width, block_width)
        lower_block = jnp.linalg.cholesky(spread(blocks[0], "row", root_row))
        solved = lower_solve(lower_block, blocks)
        first_block = jnp.where(is_root, lower_block, solved[0])
        results.append(
            jnp.concatenate([first_block[None], solved[1:]], axis=0).reshape(
                local_blocks * block_width, block_width
            )
        )
    return jnp.stack(results)[:, None]


def solution(mesh):
    return jax.shard_map(
        local,
        mesh=mesh,
        in_specs=(
            P(None, "col", "row", None),
            P("col", "row", None),
            P("col"),
            P("col", None),
            P("col", None, "row"),
            P(),
            P(),
            P(None, None, "row"),
        ),
        out_specs=P(None, "col", "row", None),
        check_vma=False,
    )
```

profile of v0, /device:TPU:1, one launch (start us, length us, event | category | flops | bytes accessed | tf_op | source)
XLA Modules:
  0.0 882.9 jit_solution(12794646725006377250)
XLA Ops:
  14.3 82.0 %all-gather.3.cloned.1.call-done = bf16[256,1,128,128]{3,2,1,0:T(8,128)(2,1)} async-done(((bf16[64,1,128,128]{3,2,1,0:T(8,128)(2,1)}), bf16[256,1,128,128]{3,2,1,0:T(8,128)(2,1)}) %all-gather.3.cloned.1.call-update) | async-done | bytes 8388624 | tf_op jit(solution)/shard_map/all_gather | solution.py:32
  100.7 6.7 broadcast_multiply_fusion.3
  107.3 9.0 %copy.179 = f32[128,128,128]{2,1,0:T(8,128)} copy(f32[128,128,128]{1,2,0:T(8,128)} %bitcast.216) | data formatting | bytes 16777216 | tf_op jit(solution)/shard_map/reshape | solution.py:45
  118.8 26.5 %scatter_fusion = f32[64,128,128]{2,1,0:T(8,128)} fusion(f32[64,128,128]{2,1,0:T(8,128)} %broadcast.191.clone.3, s32[128]{0:T(128)S(1)} %add_bitcast_fusion.3, f32[128,128,128]{2,1,0:T(8,128)} %copy.179), kind=kCustom, calls=%fused_computation.5 | custom fusion | flops 2097152 | bytes 25166336 | tf_op jit(solution)/shard_map/scatter-add | solution.py:44
  145.3 5.6 copy.253
  167.6 65.0 %reduce-scatter.5.cloned.1.call-done = f32[256,128]{0,1:T(8,128)} async-done(((f32[8192,128]{0,1:T(8,128)}), f32[256,128]{0,1:T(8,128)}) %reduce-scatter.5.cloned.1.call-update) | async-done | bytes 131088 | tf_op jit(solution)/shard_map/reduce_scatter | solution.py:65
  234.8 6.7 broadcast_multiply_fusion.2
  241.5 9.0 %copy.192 = f32[128,128,128]{2,1,0:T(8,128)} copy(f32[128,128,128]{1,2,0:T(8,128)} %bitcast.217) | data formatting | bytes 16777216 | tf_op jit(solution)/shard_map/reshape | solution.py:45
  252.9 26.5 %scatter_fusion.1 = f32[64,128,128]{2,1,0:T(8,128)} fusion(f32[64,128,128]{2,1,0:T(8,128)} %broadcast.191.clone.2, s32[128]{0:T(128)S(1)} %add_bitcast_fusion.2, f32[128,128,128]{2,1,0:T(8,128)} %copy.192), kind=kCustom, calls=%fused_computation.6 | custom fusion | flops 2097152 | bytes 25166336 | tf_op jit(solution)/shard_map/scatter-add | solution.py:44
  281.4 11.7 %cholesky.74 = f32[128,128]{1,0:T(8,128)S(1)} custom-call(f32[128,128]{1,0:T(8,128)S(1)} %fusion.19), custom_call_target="Cholesky" | custom-call | tf_op jit(solution)/shard_map/jit(cholesky)/cholesky | solution.py:75
  294.7 19.7 %custom-call.18 = f32[2,1,128,128]{2,3,1,0:T(8,128)S(1)} custom-call(f32[2,1,128,128]{3,2,1,0:T(8,128)S(1)} %select_bitcast_fusion.3), custom_call_target="InvertDiagBlocksLowerTriangular" | custom-call | tf_op jit(solution)/shard_map/triangular_solve/custom-call.0 | solution.py:13
  315.5 13.5 %psum.50 = bf16[128,128]{0,1:T(8,128)(2,1)S(1)} all-reduce(bf16[128,128]{0,1:T(8,128)(2,1)S(1)} %fusion.38), channel_id=1, replica_groups=mesh['col'=32,'row'=4] {'row'}, use_global_device_ids=true, to_apply=%region_6.9 | all-reduce | flops 16384 | bytes 65536 | tf_op jit(solution)/shard_map/psum | solution.py:9
  331.4 5.6 copy.256
  344.1 76.7 %reduce-scatter.7.cloned.1.call-done = f32[256,128]{0,1:T(8,128)} async-done(((f32[8192,128]{0,1:T(8,128)}), f32[256,128]{0,1:T(8,128)}) %reduce-scatter.7.cloned.1.call-update) | async-done | bytes 131088 | tf_op jit(solution)/shard_map/reduce_scatter | solution.py:65
  422.6 6.7 broadcast_multiply_fusion.1
  429.2 9.0 %copy.207 = f32[128,128,128]{2,1,0:T(8,128)} copy(f32[128,128,128]{1,2,0:T(8,128)} %bitcast.218) | data formatting | bytes 16777216 | tf_op jit(solution)/shard_map/reshape | solution.py:45
  440.7 26.5 %scatter_fusion.3 = f32[64,128,128]{2,1,0:T(8,128)} fusion(f32[64,128,128]{2,1,0:T(8,128)} %broadcast.191.clone.1, s32[128]{0:T(128)S(1)} %add_bitcast_fusion.1, f32[128,128,128]{2,1,0:T(8,128)} %copy.207), kind=kCustom, calls=%fused_computation.8 | custom fusion | flops 2097152 | bytes 25166336 | tf_op jit(solution)/shard_map/scatter-add | solution.py:44
  469.1 11.7 %cholesky.85 = f32[128,128]{1,0:T(8,128)S(1)} custom-call(f32[128,128]{1,0:T(8,128)S(1)} %fusion.18), custom_call_target="Cholesky" | custom-call | tf_op jit(solution)/shard_map/jit(cholesky)/cholesky | solution.py:75
  482.4 19.7 %custom-call.19 = f32[2,1,128,128]{2,3,1,0:T(8,128)S(1)} custom-call(f32[2,1,128,128]{3,2,1,0:T(8,128)S(1)} %select_bitcast_fusion.2), custom_call_target="InvertDiagBlocksLowerTriangular" | custom-call | tf_op jit(solution)/shard_map/triangular_solve/custom-call.0 | solution.py:13
  503.2 13.5 %psum.52 = bf16[128,128]{0,1:T(8,128)(2,1)S(1)} all-reduce(bf16[128,128]{0,1:T(8,128)(2,1)S(1)} %fusion.37), channel_id=1, replica_groups=mesh['col'=32,'row'=4] {'row'}, use_global_device_ids=true, to_apply=%region_11.14 | all-reduce | flops 16384 | bytes 65536 | tf_op jit(solution)/shard_map/psum | solution.py:9
  519.0 5.6 copy.259
  531.6 76.8 %reduce-scatter.9.cloned.1.call-done = f32[256,128]{0,1:T(8,128)} async-done(((f32[8192,128]{0,1:T(8,128)}), f32[256,128]{0,1:T(8,128)}) %reduce-scatter.9.cloned.1.call-update) | async-done | bytes 131088 | tf_op jit(solution)/shard_map/reduce_scatter | solution.py:65
  610.3 6.7 broadcast_multiply_fusion
  617.0 9.0 %copy.222 = f32[128,128,128]{2,1,0:T(8,128)} copy(f32[128,128,128]{1,2,0:T(8,128)} %bitcast.215) | data formatting | bytes 16777216 | tf_op jit(solution)/shard_map/reshape | solution.py:45
  628.5 26.5 %scatter_fusion.5 = f32[64,128,128]{2,1,0:T(8,128)} fusion(f32[64,128,128]{2,1,0:T(8,128)} %broadcast.191.clone, s32[128]{0:T(128)S(1)} %add_bitcast_fusion, f32[128,128,128]{2,1,0:T(8,128)} %copy.222), kind=kCustom, calls=%fused_computation.10 | custom fusion | flops 2097152 | bytes 25166336 | tf_op jit(solution)/shard_map/scatter-add | solution.py:44
  656.9 11.7 %cholesky.96 = f32[128,128]{1,0:T(8,128)S(1)} custom-call(f32[128,128]{1,0:T(8,128)S(1)} %fusion.17), custom_call_target="Cholesky" | custom-call | tf_op jit(solution)/shard_map/jit(cholesky)/cholesky | solution.py:75
  670.3 19.7 %custom-call.20 = f32[2,1,128,128]{2,3,1,0:T(8,128)S(1)} custom-call(f32[2,1,128,128]{3,2,1,0:T(8,128)S(1)} %select_bitcast_fusion.1), custom_call_target="InvertDiagBlocksLowerTriangular" | custom-call | tf_op jit(solution)/shard_map/triangular_solve/custom-call.0 | solution.py:13
  691.1 13.5 %psum.54 = bf16[128,128]{0,1:T(8,128)(2,1)S(1)} all-reduce(bf16[128,128]{0,1:T(8,128)(2,1)S(1)} %fusion.36), channel_id=1, replica_groups=mesh['col'=32,'row'=4] {'row'}, use_global_device_ids=true, to_apply=%region_16.19 | all-reduce | flops 16384 | bytes 65536 | tf_op jit(solution)/shard_map/psum | solution.py:9
  713.9 82.4 %reduce-scatter.11.cloned.1.call-done = f32[256,128]{0,1:T(8,128)} async-done(((f32[8192,128]{0,1:T(8,128)}), f32[256,128]{0,1:T(8,128)}) %reduce-scatter.11.cloned.1.call-update) | async-done | bytes 131088 | tf_op jit(solution)/shard_map/reduce_scatter | solution.py:65
  798.1 41.1 %all-reduce.11.cloned.1.call-done = f32[128,128]{0,1:T(8,128)} async-done(((f32[128,128]{0,1:T(8,128)}), f32[128,128]{0,1:T(8,128)}) %all-reduce.11.cloned.1.call-update) | async-done | bytes 65552 | tf_op jit(solution)/shard_map/psum | solution.py:9
  841.0 11.7 %cholesky.107 = f32[128,128]{1,0:T(8,128)S(1)} custom-call(f32[128,128]{1,0:T(8,128)S(1)} %fusion.16), custom_call_target="Cholesky" | custom-call | tf_op jit(solution)/shard_map/jit(cholesky)/cholesky | solution.py:75
  854.4 19.7 %custom-call.21 = f32[2,1,128,128]{2,3,1,0:T(8,128)S(1)} custom-call(f32[2,1,128,128]{3,2,1,0:T(8,128)S(1)} %select_bitcast_fusion), custom_call_target="InvertDiagBlocksLowerTriangular" | custom-call | tf_op jit(solution)/shard_map/triangular_solve/custom-call.0 | solution.py:13
  (172 shorter events, 78.9 us)
Async XLA Ops:
  6.5 3.3 copy-start.2
  6.5 3.6 copy-start
  6.5 89.8 %all-gather.3.cloned.1.call-start = ((), (), s32[]{:S(2)}) async-start(), calls=%async_computation.12 | async-start | bytes 10485760 | tf_op jit(solution)/shard_map/all_gather | solution.py:32
  9.8 222.8 %reduce-scatter.5.cloned.1.call-start = ((), (), s32[]{:S(2)}) async-start(), calls=%async_computation.4 | async-start | bytes 4325376 | tf_op jit(solution)/shard_map/reduce_scatter | solution.py:65
  10.1 3.7 copy-start.3
  150.9 0.7 copy-start.5
  150.9 10.4 %copy-start.1 = (f32[4,1,256,128]{3,2,1,0:T(8,128)S(1)}, f32[4,1,256,128]{3,2,1,0:T(8,128)}, u32[]{:S(2)}) copy-start(f32[4,1,256,128]{3,2,1,0:T(8,128)} %param.11) | copy-start | bytes 1572868
  150.9 11.8 %copy-start.4 = (s32[3,32,2]{1,2,0:T(2,128)S(1)}, s32[3,32,2]{1,2,0:T(2,128)}, u32[]{:S(2)}) copy-start(s32[3,32,2]{1,2,0:T(2,128)} %param.18) | copy-start | bytes 2308
  151.0 128.6 %all-reduce.5.cloned.1.call-start = ((), (), s32[]{:S(2)}) async-start(), calls=%async_computation.5 | async-start | bytes 131072 | tf_op jit(solution)/shard_map/psum | solution.py:9
  234.2 186.5 %reduce-scatter.7.cloned.1.call-start = ((), (), s32[]{:S(2)}) async-start(), calls=%async_computation.6 | async-start | bytes 4325376 | tf_op jit(solution)/shard_map/reduce_scatter | solution.py:65
  337.0 130.2 %all-reduce.7.cloned.1.call-start = ((), (), s32[]{:S(2)}) async-start(), calls=%async_computation.7 | async-start | bytes 131072 | tf_op jit(solution)/shard_map/psum | solution.py:9
  422.3 186.1 %reduce-scatter.9.cloned.1.call-start = ((), (), s32[]{:S(2)}) async-start(), calls=%async_computation.8 | async-start | bytes 4325376 | tf_op jit(solution)/shard_map/reduce_scatter | solution.py:65
  524.7 130.5 %all-reduce.9.cloned.1.call-start = ((), (), s32[]{:S(2)}) async-start(), calls=%async_computation.9 | async-start | bytes 131072 | tf_op jit(solution)/shard_map/psum | solution.py:9
  610.1 186.2 %reduce-scatter.11.cloned.1.call-start = ((), (), s32[]{:S(2)}) async-start(), calls=%async_computation.10 | async-start | bytes 4325376 | tf_op jit(solution)/shard_map/reduce_scatter | solution.py:65
  712.6 126.6 %all-reduce.11.cloned.1.call-start = ((), (), s32[]{:S(2)}) async-start(), calls=%async_computation.11 | async-start | bytes 131072 | tf_op jit(solution)/shard_map/psum | solution.py:9
Sparse Core Ops, SparseCore 0:
  10.0 86.3 all-gather.2
  151.1 81.5 reduce-scatter.4
  235.0 40.5 all-reduce.4
  337.1 83.5 reduce-scatter.6
  422.9 40.5 all-reduce.6
  524.8 83.6 reduce-scatter.8
  610.8 40.5 all-reduce.8
  712.7 83.5 reduce-scatter.10
  798.6 40.5 all-reduce.10
where the time goes:
time: 892 us; the launch traced here: 883 us
  waiting for transfers between devices  424 us (48%)
  other arithmetic  258 us (29%)
  local copies, waits for them, and re-layouts  102 us (11%)
  blocking collectives  40.6 us (5%)
  matrix products  28.8 us (3%)
  between operations  28.3 us (3%)
    reduce_scatter x4, waiting for transfers between devices, local(): lax.psum_scatter(slot_sums.reshape(col_count * local_blocks * block_width...  301 us
    scatter-add x4, other arithmetic, local(): jax.ops.segment_sum(source_products.reshape(src_count * local_blocks, blo...  106 us
    all_gather x1, waiting for transfers between devices, local(): column_heads = lax.all_gather(panels[:, 0][None], 'row', axis=0, tiled=True)  82 us
    another operation x9, other arithmetic, lower_solve(): lax.linalg.triangular_solve(jnp.broadcast_to(lower_block, blocks.shape),...  78.8 us
    another operation x12, other arithmetic, local(): lower_block = jnp.linalg.cholesky(spread(blocks[0], 'row', root_row))  49.9 us
    psum x4, waiting for transfers between devices, spread(): return lax.psum(block, axis)  41.2 us
    psum x3, blocking collectives, spread(): return lax.psum(block, axis)  40.6 us
    reshape x4, local copies, waits for them, and re-layouts, local(): source_products.reshape(src_count * local_blocks, block_width, block_width)  36 us
  transfers between devices with their start and end apart: 9, of which 6 were waited for; matrix products, arithmetic and copies ran while one was open for 18% of the time, Pallas kernels for 0%

commit v1 on v0

v1 whole, which is shorter than its diff:
```python
import functools

import jax
import jax.numpy as jnp
from jax import lax
from jax.experimental import pallas as pl
from jax.experimental.pallas import tpu as pltpu
from jax.sharding import PartitionSpec as P

F32 = jnp.float32
BF16 = jnp.bfloat16
B = 128
TRANS_B = (((1,), (1,)), ((), ()))
TRANS_A = (((0,), (0,)), ((), ()))
VMEM = pl.BlockSpec(memory_space=pltpu.VMEM)
SMEM = pl.BlockSpec(memory_space=pltpu.SMEM)


def cholesky_inverse(a):
    n = a.shape[0]
    lane = lax.broadcasted_iota(jnp.int32, (8, n), 1)
    sub = lax.broadcasted_iota(jnp.int32, (8, n), 0)
    upper, inverse = [], []
    w = None
    for j in range(n // 8):
        pa = a[:8]
        pw = (lane == sub + 8 * j).astype(F32)
        if w is not None:
            pw = pw + w[:8]
        pivots = jnp.zeros((8, n), F32)
        for t in range(8):
            col = jnp.broadcast_to(pa[:, 8 * j + t : 8 * j + t + 1], (8, n))
            d = jnp.broadcast_to(col[t : t + 1], (8, n))
            pivots = jnp.where(sub == t, d, pivots)
            if t < 7:
                factor = jnp.where(sub > t, col / d, 0.0)
                pa = pa - factor * pa[t : t + 1]
                pw = pw - factor * pw[t : t + 1]
        scale = lax.rsqrt(pivots)
        scale = scale * (1.5 - 0.5 * pivots * scale * scale)
        pa = jnp.where(lane >= sub + 8 * j, pa * scale, 0.0)
        pw = pw * scale
        upper.append(pa)
        inverse.append(pw)
        if j + 1 < n // 8:
            both = jnp.concatenate([pa, pw], axis=1)
            step = lax.dot_general(
                pa[:, 8 * j + 8 :] if (8 * j + 8) % 128 == 0 else pa, both, TRANS_A,
                precision=lax.Precision.HIGHEST, preferred_element_type=F32,
            )[8 * j + 8 :]
            a = a[8:] - step[:, :n]
            w = -step[:, n:] if w is None else w[8:] - step[:, n:]
    return jnp.concatenate(upper, axis=0).T, jnp.concatenate(inverse, axis=0)


def products_kernel(steps, live_ref, dest_ref, map_ref, root_ref, panel_ref, head_ref, out_ref):
    s = pl.program_id(0)
    out_ref[...] = jnp.zeros_like(out_ref)

    @pl.loop(0, live_ref[0])
    def _(i):
        dest = dest_ref[i, s]
        first = map_ref[i, s, 0]
        prod = lax.dot_general(panel_ref[i], head_ref[root_ref[i, s], i], TRANS_B, preferred_element_type=F32)
        top = pl.multiple_of(first * B, B)
        low = pl.multiple_of(B - first * B, B)
        out_ref[0, dest, pl.ds(top, B), :] += prod[:B]
        out_ref[0, dest, pl.ds(low, B), :] += prod[B:]


def slot_sums(live, dest, maps, roots, panels, heads, col_count):
    src, rows, width = panels.shape
    steps = dest.shape[1]
    return pl.pallas_call(
        functools.partial(products_kernel, steps),
        grid=(steps,),
        out_shape=jax.ShapeDtypeStruct((steps, col_count, rows, width), F32),
        in_specs=[SMEM, SMEM, SMEM, SMEM, VMEM, VMEM],
        out_specs=pl.BlockSpec((1, col_count, rows, width), lambda s: (s, 0, 0, 0)),
        name="slot_sums",
    )(live, dest, maps, roots, panels, heads)


def factor_kernel(first_step, place_ref, parent_ref, map_ref, before_ref, base_ref, diag_ref, child_ref, out_ref, low_ref, upd, dg):
    owner, is_root, row = place_ref[0], place_ref[1], place_ref[2]
    upd[...] = base_ref[...]
    dg[...] = diag_ref[...]
    if not first_step:

        @pl.loop(0, parent_ref.shape[0])
        def _(k):
            @pl.when(parent_ref[k] == owner)
            def _():
                head = child_ref[k, 2 * B :]
                prod = lax.dot_general(child_ref[k, : 2 * B], head, TRANS_B, preferred_element_type=F32)
                dg[...] -= lax.dot_general(head, head, TRANS_B, preferred_element_type=F32)
                first = map_ref[k, 0]
                top = pl.multiple_of(first * B, B)
                low = pl.multiple_of(B - first * B, B)
                upd[pl.ds(low, B), :] -= prod[B:]

                @pl.when(before_ref[k] != row)
                def _():
                    upd[pl.ds(top, B), :] -= prod[:B]

    lower, inverse = cholesky_inverse(dg[...])
    solved = lax.dot_general(
        upd[...], inverse, TRANS_B, precision=lax.Precision.HIGHEST, preferred_element_type=F32
    )
    out_ref[...] = solved

    @pl.when(is_root == 1)
    def _():
        out_ref[:B] = lower

    low_ref[...] = out_ref[...].astype(BF16)


def factor(first_step, place, parent, maps, before, base, diag, child):
    rows, width = base.shape
    return pl.pallas_call(
        functools.partial(factor_kernel, first_step),
        out_shape=[jax.ShapeDtypeStruct((rows, width), F32), jax.ShapeDtypeStruct((rows, width), BF16)],
        in_specs=[SMEM, SMEM, SMEM, SMEM, VMEM, VMEM, VMEM],
        out_specs=[VMEM, VMEM],
        scratch_shapes=[pltpu.VMEM((rows, width), F32), pltpu.VMEM((B, width), F32)],
        name="factor_first" if first_step else "factor_next",
    )(place, parent, maps, before, base, diag, child)


def local(targets, src_panels, live_counts, dest_owner, relative_map, diag_row, parent, chain_map):
    cols = lax.axis_size("col")
    owner = lax.axis_index("col")
    row = lax.axis_index("row")
    src, rows, width = src_panels.shape
    steps = targets.shape[0]
    heads = lax.all_gather(src_panels[:, :B], "row", axis=0)
    roots = diag_row[jnp.arange(steps)[None, :], dest_owner]
    sums = slot_sums(live_counts, dest_owner, relative_map, roots, src_panels, heads, cols)
    bases, diags = [], []
    for s in range(steps):
        got = lax.psum_scatter(sums[s], "col", scatter_dimension=0, tiled=False)
        base = targets[s, 0] - got
        bases.append(base)
        diags.append(lax.all_gather(base[:B], "row", axis=0)[diag_row[s, owner]])
    results = []
    child = jnp.zeros((1, 8, width), BF16)
    for s in range(steps):
        t = max(s - 1, 0)
        place = jnp.stack([owner, (diag_row[s, owner] == row).astype(jnp.int32), row])
        out, low = factor(s == 0, place, parent[t], chain_map[t], diag_row[t], bases[s], diags[s], child)
        results.append(out)
        if s + 1 < steps:
            gathered = lax.all_gather(low[B:], "row", axis=0)
            head = gathered[diag_row[s + 1, parent[s, owner]]]
            child = lax.all_gather(jnp.concatenate([low, head], axis=0), "col", axis=0)
    return jnp.stack(results)[:, None]


def solution(mesh):
    return jax.shard_map(
        local,
        mesh=mesh,
        in_specs=(
            P(None, "col", "row", None),
            P("col", "row", None),
            P("col"),
            P("col", None),
            P("col", None, "row"),
            P(),
            P(),
            P(None, None, "row"),
        ),
        out_specs=P(None, "col", "row", None),
        check_vma=False,
    )
```

time: 892 us -> 792 us (0.89)
  other arithmetic: 258 us -> 9.7 us
  Pallas kernels: 0 us -> 127 us
  waiting for transfers between devices: 424 us -> 521 us
  local copies, waits for them, and re-layouts: 102 us -> 29.7 us
  matrix products: 28.8 us -> 0 us
  blocking collectives: 40.6 us -> 67.6 us
    pallas_call x0 -> x5, Pallas kernels: none -> 127 us  [the longest x4 92.8 us: factor(): pl.pallas_call(functools.partial(factor_kernel, first_step), out_shape=[j...]
    another operation x21 -> x4, other arithmetic: 129 us -> 2.37 us  [local(): jnp.stack([owner, (diag_row[s, owner] == row).astype(jnp.int32), row])]
    scatter-add x7 -> x0, other arithmetic: 112 us -> none  [the longest x4 106 us: local(): jax.ops.segment_sum(source_products.reshape(src_count * local_blocks, blo...]
    all_gather x1 -> x4, waiting for transfers between devices: 82 us -> 180 us  [the longest x3 98.7 us: local(): child = lax.all_gather(jnp.concatenate([low, head], axis=0), 'col', axis=0)]
    all_gather x0 -> x7, blocking collectives: none -> 67.6 us  [the longest x4 38.7 us: local(): diags.append(lax.all_gather(base[:B], 'row', axis=0)[diag_row[s, owner]])]
    reshape x12 -> x0, local copies, waits for them, and re-layouts: 58.9 us -> none  [the longest x4 36 us: local(): source_products.reshape(src_count * local_blocks, block_width, block_width)]
    psum x4 -> x0, waiting for transfers between devices: 41.2 us -> none  [spread(): return lax.psum(block, axis)]
    psum x3 -> x0, blocking collectives: 40.6 us -> none  [spread(): return lax.psum(block, axis)]
  transfers between devices with their start and end apart: 9 -> 8, of which waited for: 6 -> 8; matrix products, arithmetic and copies ran while one was open for 18% -> 2% of each run, Pallas kernels for 0% -> 0%
where the time goes in v1:
time: 792 us; the launch traced here: 790 us
  waiting for transfers between devices  521 us (66%)
  Pallas kernels  127 us (16%)
  blocking collectives  67.6 us (9%)
  between operations  35.3 us (4%)
  local copies, waits for them, and re-layouts  29.7 us (4%)
  other arithmetic  9.7 us (1%)
    reduce_scatter x4, waiting for transfers between devices, local(): got = lax.psum_scatter(sums[s], 'col', scatter_dimension=0, tiled=False)  340 us
    all_gather x3, waiting for transfers between devices, local(): child = lax.all_gather(jnp.concatenate([low, head], axis=0), 'col', axis=0)  98.7 us
    pallas_call x4, Pallas kernels, factor(): pl.pallas_call(functools.partial(factor_kernel, first_step), out_shape=[j...  92.8 us
    all_gather x1, waiting for transfers between devices, local(): heads = lax.all_gather(src_panels[:, :B], 'row', axis=0)  80.9 us
    all_gather x4, blocking collectives, local(): diags.append(lax.all_gather(base[:B], 'row', axis=0)[diag_row[s, owner]])  38.7 us
    pallas_call x1, Pallas kernels, slot_sums(): pl.pallas_call(functools.partial(products_kernel, steps), grid=(steps,),...  34 us
    all_gather x3, blocking collectives, local(): gathered = lax.all_gather(low[B:], 'row', axis=0)  29 us
  transfers between devices with their start and end apart: 8, of which 8 were waited for; matrix products, arithmetic and copies ran while one was open for 2% of the time, Pallas kernels for 0%

profile of v1, /device:TPU:1, one launch (start us, length us, event | category | flops | bytes accessed | tf_op | source)
XLA Modules:
  0.0 790.4 jit_solution(11903827036714353571)
XLA Ops:
  6.5 3.2 slice.82
  9.9 0.8 copy.26.map_ref
  11.6 2.4 gather_fusion
  15.4 80.9 %all-gather.16.cloned.1.call-done = bf16[256,128,128]{2,1,0:T(8,128)(2,1)} async-done(((bf16[64,128,128]{2,1,0:T(8,128)(2,1)}), bf16[256,128,128]{2,1,0:T(8,128)(2,1)}) %all-gather.16.cloned.1.call-update) | async-done | bytes 8388624 | tf_op jit(solution)/shard_map/all_gather | solution.py:137
  96.3 34.0 %slot_sums.1 = f32[4,32,256,128]{3,2,1,0:T(8,128)} custom-call(s32[1]{0:T(128)S(6)} %copy.32.live_ref, s32[64,4]{1,0:T(8,128)} %copy.25.dest_ref, s32[64,4,2]{2,1,0:T(4,128)} %copy.26.map_ref, s32[64,4]{1,0:T(8,128)} %reshape.10.root_ref, bf16[64,256,128]{2,1,0:T(8,128)(2,1)} %panel_ref.1, bf16[4,64,128,128]{3,2,1,0:T(8,128)(2,1)} %bitcast.97), custom_call_target="tpu_custom_call" | custom-call | tf_op jit(solution)/shard_map/slot_sums/pallas_call | solution.py:74
  130.2 12.2 %slice_bitcast_fusion.3 = (f32[32,256,128]{2,1,0:T(8,128)}, f32[32,256,128]{2,1,0:T(8,128)}, f32[32,256,128]{2,1,0:T(8,128)}, f32[32,256,128]{2,1,0:T(8,128)}) fusion(f32[4,32,256,128]{3,2,1,0:T(8,128)} %slot_sums.1), kind=kLoop, calls=%fused_computation.4 | loop fusion | bytes 33554432 | tf_op jit(solution)/shard_map/squeeze | solution.py:142
  157.6 83.8 %reduce-scatter.11.cloned.1.call-done = f32[1,256,128]{2,1,0:T(8,128)} async-done(((f32[32,256,128]{2,1,0:T(8,128)}), f32[1,256,128]{2,1,0:T(8,128)}) %reduce-scatter.11.cloned.1.call-update) | async-done | bytes 131088 | tf_op jit(solution)/shard_map/reduce_scatter | solution.py:142
  241.5 85.3 %reduce-scatter.5.cloned.1.call-done = f32[1,256,128]{2,1,0:T(8,128)} async-done(((f32[32,256,128]{2,1,0:T(8,128)}), f32[1,256,128]{2,1,0:T(8,128)}) %reduce-scatter.5.cloned.1.call-update) | async-done | bytes 131088 | tf_op jit(solution)/shard_map/reduce_scatter | solution.py:142
  326.8 85.2 %reduce-scatter.7.cloned.1.call-done = f32[1,256,128]{2,1,0:T(8,128)} async-done(((f32[32,256,128]{2,1,0:T(8,128)}), f32[1,256,128]{2,1,0:T(8,128)}) %reduce-scatter.7.cloned.1.call-update) | async-done | bytes 131088 | tf_op jit(solution)/shard_map/reduce_scatter | solution.py:142
  412.0 85.2 %reduce-scatter.9.cloned.1.call-done = f32[1,256,128]{2,1,0:T(8,128)} async-done(((f32[32,256,128]{2,1,0:T(8,128)}), f32[1,256,128]{2,1,0:T(8,128)}) %reduce-scatter.9.cloned.1.call-update) | async-done | bytes 131088 | tf_op jit(solution)/shard_map/reduce_scatter | solution.py:142
  497.2 1.1 bitcast_subtract_fusion.3
  498.4 9.9 %all-gather.1 = f32[512,128]{1,0:T(8,128)S(1)} all-gather(f32[128,128]{1,0:T(8,128)S(1)} %slice.106), channel_id=3, replica_groups=mesh['col'=32,'row'=4] {'row'}, dimensions={0}, use_global_device_ids=true | all-gather | bytes 327680 | tf_op jit(solution)/shard_map/all_gather | solution.py:145
  509.4 22.0 %factor_first.1 = (f32[256,128]{1,0:T(8,128)}, bf16[256,128]{1,0:T(8,128)(2,1)}) custom-call(s32[3]{0:T(128)} %add_add_fusion.place_ref, s32[32]{0:T(128)} %get-tuple-element.48.parent_ref, s32[32,2]{1,0:T(8,128)} %copy.27.map_ref, s32[32]{0:T(128)} %get-tuple-element.40.before_ref, f32[256,128]{1,0:T(8,128)} %copy-done.1, ...), custom_call_target="tpu_custom_call" | custom-call | tf_op jit(solution)/shard_map/factor_first/pallas_call | solution.py:121
  531.4 0.8 slice.88
  532.2 9.1 %all-gather.3 = bf16[512,128]{1,0:T(8,128)(2,1)S(1)} all-gather(bf16[128,128]{1,0:T(8,128)(2,1)S(1)} %slice.88), channel_id=5, replica_groups=mesh['col'=32,'row'=4] {'row'}, dimensions={0}, use_global_device_ids=true | all-gather | bytes 163840 | tf_op jit(solution)/shard_map/all_gather | solution.py:154
  541.3 1.5 pad_maximum_fusion
  547.9 9.4 %all-gather.2 = f32[512,128]{1,0:T(8,128)S(1)} all-gather(f32[128,128]{1,0:T(8,128)S(1)} %slice.108), channel_id=4, replica_groups=mesh['col'=32,'row'=4] {'row'}, dimensions={0}, use_global_device_ids=true | all-gather | bytes 327680 | tf_op jit(solution)/shard_map/all_gather | solution.py:145
  557.9 36.3 %all-gather.18.cloned.1.call-done = bf16[12288,128]{1,0:T(8,128)(2,1)} async-done(((bf16[384,128]{1,0:T(8,128)(2,1)}), bf16[12288,128]{1,0:T(8,128)(2,1)}) %all-gather.18.cloned.1.call-update) | async-done | bytes 3145744 | tf_op jit(solution)/shard_map/all_gather | solution.py:156
  594.2 23.9 %factor_next.3 = (f32[256,128]{1,0:T(8,128)}, bf16[256,128]{1,0:T(8,128)(2,1)}) custom-call(s32[3]{0:T(128)} %add_add_fusion.1.place_ref, s32[32]{0:T(128)} %get-tuple-element.48.parent_ref, s32[32,2]{1,0:T(8,128)} %copy.27.map_ref, s32[32]{0:T(128)} %get-tuple-element.40.before_ref, f32[256,128]{1,0:T(8,128)} %copy-done.4, ...), custom_call_target="tpu_custom_call" | custom-call | tf_op jit(solution)/shard_map/factor_next/pallas_call | solution.py:121
  618.1 0.8 slice.95
  618.9 9.9 %all-gather.6 = bf16[512,128]{1,0:T(8,128)(2,1)S(1)} all-gather(bf16[128,128]{1,0:T(8,128)(2,1)S(1)} %slice.95), channel_id=8, replica_groups=mesh['col'=32,'row'=4] {'row'}, dimensions={0}, use_global_device_ids=true | all-gather | bytes 163840 | tf_op jit(solution)/shard_map/all_gather | solution.py:154
  628.8 1.5 pad_maximum_fusion.1
  636.1 10.1 %all-gather.5 = f32[512,128]{1,0:T(8,128)S(1)} all-gather(f32[128,128]{1,0:T(8,128)S(1)} %slice.110), channel_id=7, replica_groups=mesh['col'=32,'row'=4] {'row'}, dimensions={0}, use_global_device_ids=true | all-gather | bytes 327680 | tf_op jit(solution)/shard_map/all_gather | solution.py:145
  646.8 29.8 %all-gather.20.cloned.1.call-done = bf16[12288,128]{1,0:T(8,128)(2,1)} async-done(((bf16[384,128]{1,0:T(8,128)(2,1)}), bf16[12288,128]{1,0:T(8,128)(2,1)}) %all-gather.20.cloned.1.call-update) | async-done | bytes 3145744 | tf_op jit(solution)/shard_map/all_gather | solution.py:156
  676.6 23.6 %factor_next.4 = (f32[256,128]{1,0:T(8,128)}, bf16[256,128]{1,0:T(8,128)(2,1)}) custom-call(s32[3]{0:T(128)} %add_add_fusion.2.place_ref, s32[32]{0:T(128)} %get-tuple-element.47.parent_ref, s32[32,2]{1,0:T(8,128)} %copy.29.map_ref, s32[32]{0:T(128)} %get-tuple-element.41.before_ref, f32[256,128]{1,0:T(8,128)} %copy-done.3, ...), custom_call_target="tpu_custom_call" | custom-call | tf_op jit(solution)/shard_map/factor_next/pallas_call | solution.py:121
  700.2 0.8 slice.102
  700.9 9.9 %all-gather.9 = bf16[512,128]{1,0:T(8,128)(2,1)S(1)} all-gather(bf16[128,128]{1,0:T(8,128)(2,1)S(1)} %slice.102), channel_id=11, replica_groups=mesh['col'=32,'row'=4] {'row'}, dimensions={0}, use_global_device_ids=true | all-gather | bytes 163840 | tf_op jit(solution)/shard_map/all_gather | solution.py:154
  710.9 1.5 pad_maximum_fusion.2
  715.9 9.4 %all-gather.8 = f32[512,128]{1,0:T(8,128)S(1)} all-gather(f32[128,128]{1,0:T(8,128)S(1)} %slice.112), channel_id=10, replica_groups=mesh['col'=32,'row'=4] {'row'}, dimensions={0}, use_global_device_ids=true | all-gather | bytes 327680 | tf_op jit(solution)/shard_map/all_gather | solution.py:145
  725.9 32.6 %all-gather.22.cloned.1.call-done = bf16[12288,128]{1,0:T(8,128)(2,1)} async-done(((bf16[384,128]{1,0:T(8,128)(2,1)}), bf16[12288,128]{1,0:T(8,128)(2,1)}) %all-gather.22.cloned.1.call-update) | async-done | bytes 3145744 | tf_op jit(solution)/shard_map/all_gather | solution.py:156
  758.4 23.4 %factor_next.5 = (f32[256,128]{1,0:T(8,128)}, bf16[256,128]{1,0:T(8,128)(2,1)}) custom-call(s32[3]{0:T(128)} %add_add_fusion.3.place_ref, s32[32]{0:T(128)} %get-tuple-element.46.parent_ref, s32[32,2]{1,0:T(8,128)} %copy.30.map_ref, s32[32]{0:T(128)} %get-tuple-element.42.before_ref, f32[256,128]{1,0:T(8,128)} %copy-done.2, ...), custom_call_target="tpu_custom_call" | custom-call | tf_op jit(solution)/shard_map/factor_next/pallas_call | solution.py:121
  781.8 1.7 maximum_bitcast_fusion
  (70 shorter events, 13.2 us)
Async XLA Ops:
  6.5 3.3 copy-start.11
  6.5 4.1 copy-start.9
  6.5 5.0 copy-start
  6.5 89.7 %all-gather.16.cloned.1.call-start = ((), (), s32[]{:S(2)}) async-start(), calls=%async_computation.8 | async-start | bytes 10485760 | tf_op jit(solution)/shard_map/all_gather | solution.py:137
  9.8 231.7 %reduce-scatter.11.cloned.1.call-start = ((), (), s32[]{:S(2)}) async-start(), calls=%async_computation.7 | async-start | bytes 4325376 | tf_op jit(solution)/shard_map/reduce_scatter | solution.py:142
  142.5 184.3 %reduce-scatter.5.cloned.1.call-start = ((), (), s32[]{:S(2)}) async-start(), calls=%async_computation.4 | async-start | bytes 4325376 | tf_op jit(solution)/shard_map/reduce_scatter | solution.py:142
  143.2 268.8 %reduce-scatter.7.cloned.1.call-start = ((), (), s32[]{:S(2)}) async-start(), calls=%async_computation.5 | async-start | bytes 4325376 | tf_op jit(solution)/shard_map/reduce_scatter | solution.py:142
  143.2 1.2 copy-start.10
  143.3 11.2 %copy-start.12 = (s32[3,32,2]{1,2,0:T(2,128)S(1)}, s32[3,32,2]{1,2,0:T(2,128)}, u32[]{:S(2)}) copy-start(s32[3,32,2]{1,2,0:T(2,128)} %param.15) | copy-start | bytes 2308
  143.3 353.9 %copy-start.5 = (f32[4,1,256,128]{3,2,1,0:T(8,128)S(1)}, f32[4,1,256,128]{3,2,1,0:T(8,128)}, u32[]{:S(2)}) copy-start(f32[4,1,256,128]{3,2,1,0:T(8,128)} %param.8) | copy-start | bytes 1572868
  143.8 353.4 %reduce-scatter.9.cloned.1.call-start = ((), (), s32[]{:S(2)}) async-start(), calls=%async_computation.6 | async-start | bytes 4325376 | tf_op jit(solution)/shard_map/reduce_scatter | solution.py:142
  144.4 449.8 %all-gather.18.cloned.1.call-start = ((), (), s32[]{:S(2)}) async-start(), calls=%async_computation.9 | async-start | bytes 3244032 | tf_op jit(solution)/shard_map/all_gather | solution.py:156
  498.3 11.1 %copy-start.1 = (f32[256,128]{1,0:T(8,128)}, f32[256,128]{1,0:T(8,128)S(1)}, u32[]{:S(2)}) copy-start(f32[256,128]{1,0:T(8,128)S(1)} %get-tuple-element.23.base_ref) | copy-start | bytes 393220
  498.3 95.8 %copy-start.4 = (f32[256,128]{1,0:T(8,128)}, f32[256,128]{1,0:T(8,128)S(1)}, u32[]{:S(2)}) copy-start(f32[256,128]{1,0:T(8,128)S(1)} %get-tuple-element.24.base_ref) | copy-start | bytes 393220
  498.3 178.2 %copy-start.3 = (f32[256,128]{1,0:T(8,128)}, f32[256,128]{1,0:T(8,128)S(1)}, u32[]{:S(2)}) copy-start(f32[256,128]{1,0:T(8,128)S(1)} %get-tuple-element.26.base_ref) | copy-start | bytes 393220
  498.4 217.5 %copy-start.2 = (f32[256,128]{1,0:T(8,128)}, f32[256,128]{1,0:T(8,128)S(1)}, u32[]{:S(2)}) copy-start(f32[256,128]{1,0:T(8,128)S(1)} %get-tuple-element.25.base_ref) | copy-start | bytes 393220
  542.8 133.8 %all-gather.20.cloned.1.call-start = ((), (), s32[]{:S(2)}) async-start(), calls=%async_computation.10 | async-start | bytes 3244032 | tf_op jit(solution)/shard_map/all_gather | solution.py:156
  630.3 128.1 %all-gather.22.cloned.1.call-start = ((), (), s32[]{:S(2)}) async-start(), calls=%async_computation.11 | async-start | bytes 3244032 | tf_op jit(solution)/shard_map/all_gather | solution.py:156
  636.1 145.7 %copy-start.6 = (f32[256,128]{1,0:T(8,128)S(1)}, f32[256,128]{1,0:T(8,128)}, u32[]{:S(2)}) copy-start(f32[256,128]{1,0:T(8,128)} %get-tuple-element.12) | copy-start | bytes 393220
  636.1 145.7 %copy-start.7 = (f32[256,128]{1,0:T(8,128)S(1)}, f32[256,128]{1,0:T(8,128)}, u32[]{:S(2)}) copy-start(f32[256,128]{1,0:T(8,128)} %get-tuple-element.14) | copy-start | bytes 393220
  700.1 81.6 %copy-start.8 = (f32[256,128]{1,0:T(8,128)S(1)}, f32[256,128]{1,0:T(8,128)}, u32[]{:S(2)}) copy-start(f32[256,128]{1,0:T(8,128)} %get-tuple-element.16) | copy-start | bytes 393220
Sparse Core Ops, SparseCore 0:
  9.9 86.3 all-gather.15
  142.6 98.8 reduce-scatter.10
  245.1 81.6 reduce-scatter.4
  330.3 81.6 reduce-scatter.6
  415.5 81.6 reduce-scatter.8
  542.9 51.2 all-gather.17
  630.4 46.1 all-gather.19
  712.5 45.8 all-gather.21

commit v2 on v1

--- a/solution.py
+++ b/solution.py
@@ -13,6 +13,7 @@
 TRANS_B = (((1,), (1,)), ((), ()))
 TRANS_A = (((0,), (0,)), ((), ()))
 VMEM = pl.BlockSpec(memory_space=pltpu.VMEM)
+MESH = pl.DeviceIdType.MESH
 SMEM = pl.BlockSpec(memory_space=pltpu.SMEM)
 
 
@@ -91,8 +92,9 @@
         def _(k):
             @pl.when(parent_ref[k] == owner)
             def _():
-                head = child_ref[k, 2 * B :]
-                prod = lax.dot_general(child_ref[k, : 2 * B], head, TRANS_B, preferred_element_type=F32)
+                parts = [child_ref[h, k, b] for b in range(3) for h in range(2)]
+                head = jnp.concatenate(parts[4:], axis=0)
+                prod = lax.dot_general(jnp.concatenate(parts[:4], axis=0), head, TRANS_B, preferred_element_type=F32)
                 dg[...] -= lax.dot_general(head, head, TRANS_B, preferred_element_type=F32)
                 first = map_ref[k, 0]
                 top = pl.multiple_of(first * B, B)
@@ -116,44 +118,254 @@
     low_ref[...] = out_ref[...].astype(BF16)
 
 
-def factor(first_step, place, parent, maps, before, base, diag, child):
-    rows, width = base.shape
+def factor(step, place, parent, maps, before, base, diag, child):
+    rows, width = base.shape[1:]
     return pl.pallas_call(
-        functools.partial(factor_kernel, first_step),
+        functools.partial(factor_kernel, step == 0),
+        grid=(1,),
         out_shape=[jax.ShapeDtypeStruct((rows, width), F32), jax.ShapeDtypeStruct((rows, width), BF16)],
-        in_specs=[SMEM, SMEM, SMEM, SMEM, VMEM, VMEM, VMEM],
+        in_specs=[
+            SMEM, SMEM, SMEM, SMEM,
+            pl.BlockSpec((None, rows, width), lambda i: (step, 0, 0)),
+            pl.BlockSpec((None, B, width), lambda i: (step, 0, 0)),
+            VMEM,
+        ],
         out_specs=[VMEM, VMEM],
         scratch_shapes=[pltpu.VMEM((rows, width), F32), pltpu.VMEM((B, width), F32)],
-        name="factor_first" if first_step else "factor_next",
+        name="factor_first" if step == 0 else "factor_next",
     )(place, parent, maps, before, base, diag, child)
+
+
+def position():
+    me = lax.axis_index("col")
+    return me // 8, lax.rem(me // 2, 4), lax.rem(me, 2), lax.axis_index("row")
+
+
+def at_x(d):
+    x, y, p, _ = position()
+    return lax.rem(x + d, 4), {"col": (lax.rem(x + d, 4) * 4 + y) * 2 + p}
+
+
+def at_y(d):
+    x, y, p, _ = position()
+    return lax.rem(y + d, 4), {"col": (x * 4 + lax.rem(y + d, 4)) * 2 + p}
+
+
+def at_z(d):
+    return {"row": lax.rem(lax.axis_index("row") + d, 4)}
+
+
+def partner():
+    x, y, p, _ = position()
+    return {"col": (x * 4 + y) * 2 + 1 - p}
+
+
+def greet():
+    barrier = pltpu.get_barrier_semaphore()
+    peers = [partner()] + [at_z(d) for d in (1, 2, 3)] + [f(d)[1] for f in (at_x, at_y) for d in (1, 2, 3)]
+    for peer in peers:
+        pl.semaphore_signal(barrier, inc=1, device_id=peer, device_id_type=MESH)
+    pl.semaphore_wait(barrier, len(peers))
+
+
+class Copies:
+    def __init__(self, send, recv):
+        self.send, self.recv, self.all = send, recv, []
+
+    def start(self, src, dst, peer):
+        n = len(self.all)
+        copy = pltpu.make_async_remote_copy(
+            src_ref=src, dst_ref=dst, send_sem=self.send.at[n], recv_sem=self.recv.at[n], device_id=peer, device_id_type=MESH
+        )
+        copy.start()
+        self.all.append(copy)
+        return copy
+
+    def finish(self):
+        for copy in self.all:
+            copy.wait_send()
+
+
+def scatter_kernel(root_ref, sums, target_ref, base_ref, diag_ref, acc, in0, part, in1, in2, zbuf, load_sem, send_sem, recv_sem):
+    steps = sums.shape[0]
+    x, y, p, row = position()
+    copies = Copies(send_sem, recv_sem)
+    loads, first, second, third, fourth = {}, {}, {}, {}, {}
+    for s in range(steps):
+        loads[s] = pltpu.make_async_copy(sums.at[s, :, :, p], acc.at[s], load_sem.at[s])
+        loads[s].start()
+    greet()
+    for s in range(steps):
+        first[s] = copies.start(sums.at[s, :, :, 1 - p], in0.at[s], partner())
+
+    def pair(s):
+        loads[s].wait()
+        first[s].wait_recv()
+
+        @pl.loop(0, 16)
+        def _(i):
+            acc[s, i // 4, lax.rem(i, 4)] += in0[s, i // 4, lax.rem(i, 4)]
+
+        second[s] = []
+        for d in (2, 1, 3):
+            to, peer = at_x(d)
+            second[s].append(copies.start(acc.at[s, to, :, :B], in1.at[s, 0, d - 1], peer))
+            to, peer = at_y(d)
+            second[s].append(copies.start(acc.at[s, :, to, B:], in1.at[s, 1, d - 1], peer))
+
+    def cross(s):
+        for copy in second[s]:
+            copy.wait_recv()
+
+        @pl.loop(0, 4)
+        def _(i):
+            part[s, 0, i] = acc[s, x, i, :B] + in1[s, 0, 0, i] + in1[s, 0, 1, i] + in1[s, 0, 2, i]
+            part[s, 1, i] = acc[s, i, y, B:] + in1[s, 1, 0, i] + in1[s, 1, 1, i] + in1[s, 1, 2, i]
+
+        third[s] = []
+        for d in (2, 1, 3):
+            to, peer = at_y(d)
+            third[s].append(copies.start(part.at[s, 0, to], in2.at[s, 0, d - 1], peer))
+            to, peer = at_x(d)
+            third[s].append(copies.start(part.at[s, 1, to], in2.at[s, 1, d - 1], peer))
+
+    def finish(s):
+        for copy in third[s]:
+            copy.wait_recv()
+        base = target_ref[s, :B] - (part[s, 0, y] + in2[s, 0, 0] + in2[s, 0, 1] + in2[s, 0, 2])
+        base_ref[s, :B] = base
+        zbuf[s, row] = base
+        base_ref[s, B:] = target_ref[s, B:] - (part[s, 1, x] + in2[s, 1, 0] + in2[s, 1, 1] + in2[s, 1, 2])
+        fourth[s] = [copies.start(zbuf.at[s, row], zbuf.at[s, row], at_z(d)) for d in (2, 1, 3)]
+
+    for t in range(steps + 2):
+        if t < steps:
+            pair(t)
+        if 0 <= t - 1 < steps:
+            cross(t - 1)
+        if 0 <= t - 2 < steps:
+            finish(t - 2)
+    for s in range(steps):
+        for copy in fourth[s]:
+            copy.wait_recv()
+    for s in range(steps):
+        diag_ref[s] = zbuf[s, root_ref[s]]
+    copies.finish()
+
+
+def scatter_reduce(roots, sums, targets):
+    steps, rows, width = targets.shape
+    count = steps * 16
+    return pl.pallas_call(
+        scatter_kernel,
+        out_shape=[jax.ShapeDtypeStruct((steps, rows, width), F32), jax.ShapeDtypeStruct((steps, B, width), F32)],
+        in_specs=[SMEM, pl.BlockSpec(memory_space=pl.ANY), VMEM],
+        out_specs=[VMEM, VMEM],
+        scratch_shapes=[
+            pltpu.VMEM((steps, 4, 4, rows, width), F32),
+            pltpu.VMEM((steps, 4, 4, rows, width), F32),
+            pltpu.VMEM((steps, 2, 4, B, width), F32),
+            pltpu.VMEM((steps, 2, 3, 4, B, width), F32),
+            pltpu.VMEM((steps, 2, 3, B, width), F32),
+            pltpu.VMEM((steps, 4, B, width), F32),
+            pltpu.SemaphoreType.DMA((steps,)),
+            pltpu.SemaphoreType.DMA((count,)),
+            pltpu.SemaphoreType.DMA((count,)),
+        ],
+        compiler_params=pltpu.CompilerParams(collective_id=0, has_side_effects=True),
+        name="scatter_reduce",
+    )(roots, sums.reshape(steps, 4, 4, 2, rows, width), targets)
+
+
+def exchange_kernel(root_ref, low, out, zbuf, send_sem, recv_sem):
+    x, y, p, row = position()
+    copies = Copies(send_sem, recv_sem)
+    for h in range(2):
+        out[h, x, y, p, :2] = low[:, h]
+    zbuf[row] = low[1]
+    greet()
+    rows, head = slice(0, 2), slice(2, 3)
+    heads = [copies.start(low.at[1], zbuf.at[row], at_z(d)) for d in (2, 1, 3)]
+
+    def open_half(h, what, src):
+        move = at_y if h else at_x
+        return [copies.start(src, out.at[h, x, y, p, what], move(d)[1]) for d in (2, 1, 3)]
+
+    def line(h, fixed, what):
+        return out.at[1, fixed, :, p, what] if h else out.at[0, :, fixed, p, what]
+
+    def turn(h, what, opened):
+        for copy in opened:
+            copy.wait_recv()
+        move, here = (at_x, x) if h else (at_y, y)
+        ref = line(h, here, what)
+        return [copies.start(ref, ref, move(d)[1]) for d in (2, 1, 3)], copies.start(ref, ref, partner())
+
+    def close(h, what, turned):
+        done = [turned[1]]
+        move = at_x if h else at_y
+        for d, copy in zip((2, 1, 3), turned[0]):
+            copy.wait_recv()
+            ref = line(h, move(4 - d)[0], what)
+            done.append(copies.start(ref, ref, partner()))
+        return done
+
+    opened = [open_half(h, rows, low.at[:, h]) for h in range(2)]
+    for copy in heads:
+        copy.wait_recv()
+    picked = zbuf[root_ref[0]]
+    for h in range(2):
+        out[h, x, y, p, 2] = picked[h]
+    opened_head = [open_half(h, head, out.at[h, x, y, p, head]) for h in range(2)]
+    turned = [turn(h, rows, opened[h]) for h in range(2)]
+    turned_head = [turn(h, head, opened_head[h]) for h in range(2)]
+    done = []
+    for h in range(2):
+        done += close(h, rows, turned[h])
+    for h in range(2):
+        done += close(h, head, turned_head[h])
+    for copy in done:
+        copy.wait_recv()
+    copies.finish()
+
+
+def exchange(root, low):
+    width = low.shape[1]
+    out = pl.pallas_call(
+        exchange_kernel,
+        out_shape=jax.ShapeDtypeStruct((2, 4, 4, 2, 3, B // 2, width), BF16),
+        in_specs=[SMEM, VMEM],
+        out_specs=VMEM,
+        scratch_shapes=[
+            pltpu.VMEM((4, 2, B // 2, width), BF16),
+            pltpu.SemaphoreType.DMA((43,)),
+            pltpu.SemaphoreType.DMA((43,)),
+        ],
+        compiler_params=pltpu.CompilerParams(collective_id=1, has_side_effects=True),
+        name="exchange",
+    )(root, low.reshape(2, 2, B // 2, width))
+    return out.reshape(2, 32, 3, B // 2, width)
 
 
 def local(targets, src_panels, live_counts, dest_owner, relative_map, diag_row, parent, chain_map):
     cols = lax.axis_size("col")
     owner = lax.axis_index("col")
     row = lax.axis_index("row")
-    src, rows, width = src_panels.shape
+    width = src_panels.shape[2]
     steps = targets.shape[0]
     heads = lax.all_gather(src_panels[:, :B], "row", axis=0)
     roots = diag_row[jnp.arange(steps)[None, :], dest_owner]
     sums = slot_sums(live_counts, dest_owner, relative_map, roots, src_panels, heads, cols)
-    bases, diags = [], []
-    for s in range(steps):
-        got = lax.psum_scatter(sums[s], "col", scatter_dimension=0, tiled=False)
-        base = targets[s, 0] - got
-        bases.append(base)
-        diags.append(lax.all_gather(base[:B], "row", axis=0)[diag_row[s, owner]])
+    base, diag = scatter_reduce(diag_row[:, owner], sums, targets[:, 0])
     results = []
-    child = jnp.zeros((1, 8, width), BF16)
+    child = jnp.zeros((2, 1, 3, 8, width), BF16)
     for s in range(steps):
         t = max(s - 1, 0)
         place = jnp.stack([owner, (diag_row[s, owner] == row).astype(jnp.int32), row])
-        out, low = factor(s == 0, place, parent[t], chain_map[t], diag_row[t], bases[s], diags[s], child)
+        out, low = factor(s, place, parent[t], chain_map[t], diag_row[t], base, diag, child)
         results.append(out)
         if s + 1 < steps:
-            gathered = lax.all_gather(low[B:], "row", axis=0)
-            head = gathered[diag_row[s + 1, parent[s, owner]]]
-            child = lax.all_gather(jnp.concatenate([low, head], axis=0), "col", axis=0)
+            child = exchange(diag_row[s + 1, parent[s, owner]].reshape(1), low)
     return jnp.stack(results)[:, None]
 
 

time: 792 us -> 394 us (0.50)
  waiting for transfers between devices: 521 us -> 66.7 us
  Pallas kernels: 127 us -> 288 us
  blocking collectives: 67.6 us -> 0 us
  local copies, waits for them, and re-layouts: 29.7 us -> 13.4 us
  between operations: 35.3 us -> 22.4 us
    reduce_scatter x4 -> x0, waiting for transfers between devices: 340 us -> none  [local(): got = lax.psum_scatter(sums[s], 'col', scatter_dimension=0, tiled=False)]
    pallas_call x4 -> x8, Pallas kernels: 92.8 us -> 235 us  [the longest x4 93 us: factor(): pl.pallas_call(functools.partial(factor_kernel, step == 0), grid=(1,), ou...]
    all_gather x3 -> x0, waiting for transfers between devices: 98.7 us -> none  [local(): child = lax.all_gather(jnp.concatenate([low, head], axis=0), 'col', axis=0)]
    all_gather x7 -> x0, blocking collectives: 67.6 us -> none  [the longest x4 38.7 us: local(): diags.append(lax.all_gather(base[:B], 'row', axis=0)[diag_row[s, owner]])]
    pallas_call x1, Pallas kernels: 34 us -> 53 us  [slot_sums(): pl.pallas_call(functools.partial(products_kernel, steps), grid=(steps,),...]
    squeeze x8 -> x0, local copies, waits for them, and re-layouts: 14.7 us -> none  [the longest x1 12.2 us: local(): got = lax.psum_scatter(sums[s], 'col', scatter_dimension=0, tiled=False)]
    all_gather x1, waiting for transfers between devices: 80.9 us -> 66.7 us  [local(): heads = lax.all_gather(src_panels[:, :B], 'row', axis=0)]
  transfers between devices with their start and end apart: 8 -> 1, of which waited for: 8 -> 1; matrix products, arithmetic and copies ran while one was open for 2% -> 3% of each run, Pallas kernels for 0% -> 0%
where the time goes in v2:
time: 394 us
  Pallas kernels  288 us (73%)
  waiting for transfers between devices  66.7 us (17%)
  between operations  22.4 us (6%)
  local copies, waits for them, and re-layouts  13.4 us (3%)
    pallas_call x4, Pallas kernels, factor(): pl.pallas_call(functools.partial(factor_kernel, step == 0), grid=(1,), ou...  93 us
    pallas_call x1, Pallas kernels, scatter_reduce(): pl.pallas_call(scatter_kernel, out_shape=[jax.ShapeDtypeStruct((steps, ro...  73.6 us
    pallas_call x3, Pallas kernels, exchange(): pl.pallas_call(exchange_kernel, out_shape=jax.ShapeDtypeStruct((2, 4, 4,...  68.4 us
    all_gather x1, waiting for transfers between devices, local(): heads = lax.all_gather(src_panels[:, :B], 'row', axis=0)  66.7 us
    pallas_call x1, Pallas kernels, slot_sums(): pl.pallas_call(functools.partial(products_kernel, steps), grid=(steps,),...  53 us
  transfers between devices with their start and end apart: 1, of which 1 were waited for; matrix products, arithmetic and copies ran while one was open for 3% of the time, Pallas kernels for 0%

profile of v2, /device:TPU:1, one launch (start us, length us, event | category | flops | bytes accessed | tf_op | source)
XLA Modules:
  0.0 393.6 jit_solution(8481473365643066303)
XLA Ops:
  6.5 0.0 all-gather.3.cloned.1.call-start
  6.6 3.2 slice.36
  9.8 0.0 all-gather.3.cloned.1.call-update
  9.8 0.6 constant_dynamic-slice_fusion.6
  14.3 0.8 dynamic-slice_reduce_fusion.root_ref
  17.0 0.7 constant_dynamic-slice_fusion.7
  19.0 0.0 copy-done.6
  19.0 0.8 copy.26.map_ref
  19.8 0.7 copy.25.dest_ref
  20.5 0.1 copy.24
  20.6 0.1 reshape.35
  20.7 0.0 copy-start.7
  20.7 2.4 gather_fusion
  23.2 0.7 reshape.38.root_ref
  24.6 0.7 copy.27.map_ref
  26.4 0.7 copy.29.map_ref
  27.1 0.7 copy.30.map_ref
  27.8 0.6 add_add_fusion
  28.4 0.6 add_add_fusion.2
  29.0 0.6 slice_bitcast_fusion.7
  29.6 66.7 %all-gather.3.cloned.1.call-done = bf16[256,128,128]{2,1,0:T(8,128)(2,1)} async-done(((bf16[64,128,128]{2,1,0:T(8,128)(2,1)}), bf16[256,128,128]{2,1,0:T(8,128)(2,1)}) %all-gather.3.cloned.1.call-update) | async-done | bytes 8388624 | tf_op jit(solution)/shard_map/all_gather | solution.py:356
  96.3 53.0 %slot_sums.1 = f32[4,32,256,128]{3,2,1,0:T(8,128)} custom-call(s32[1]{0:T(128)S(6)} %copy.32.live_ref, s32[64,4]{1,0:T(8,128)} %copy.25.dest_ref, s32[64,4,2]{2,1,0:T(4,128)} %copy.26.map_ref, s32[64,4]{1,0:T(8,128)} %reshape.38.root_ref, bf16[64,256,128]{2,1,0:T(8,128)(2,1)} %panel_ref.1, bf16[4,64,128,128]{3,2,1,0:T(8,128)(2,1)} %bitcast.61), custom_call_target="tpu_custom_call" | custom-call | tf_op jit(solution)/shard_map/slot_sums/pallas_call | solution.py:75
  149.3 73.6 %scatter_reduce.1 = (f32[4,256,128]{2,1,0:T(8,128)}, f32[4,128,128]{2,1,0:T(8,128)}) custom-call(s32[4]{0:T(128)} %dynamic-slice_reduce_fusion.root_ref, f32[4,4,4,2,256,128]{5,4,3,2,1,0:T(8,128)} %bitcast.57, f32[4,256,128]{2,1,0:T(8,128)} %bitcast.62), custom_call_target="tpu_custom_call" | custom-call | tf_op jit(solution)/shard_map/scatter_reduce/pallas_call | solution.py:259
  223.0 0.6 broadcast_in_dim.17.child_ref
  223.6 21.9 %factor_first.1 = (f32[256,128]{1,0:T(8,128)}, bf16[256,128]{1,0:T(8,128)(2,1)}) custom-call(s32[3]{0:T(128)} %get-tuple-element.42.place_ref, s32[32]{0:T(128)} %get-tuple-element.48.parent_ref, s32[32,2]{1,0:T(8,128)} %copy.27.map_ref, s32[32]{0:T(128)} %get-tuple-element.36.before_ref, f32[4,256,128]{2,1,0:T(8,128)} %get-tuple-element.14.base_ref, ...), custom_call_target="tpu_custom_call" | custom-call | tf_op jit(solution)/shard_map/factor_first/pallas_call | solution.py:123
  245.5 23.6 %exchange.3 = bf16[2,4,4,2,3,64,128]{6,5,4,3,2,1,0:T(8,128)(2,1)} custom-call(s32[1]{0:T(128)} %bitcast.15.root_ref, bf16[2,2,64,128]{3,2,1,0:T(8,128)(2,1)} %bitcast.69), custom_call_target="tpu_custom_call" | custom-call | tf_op jit(solution)/shard_map/exchange/pallas_call | solution.py:334
  269.1 23.5 %factor_next.3 = (f32[256,128]{1,0:T(8,128)}, bf16[256,128]{1,0:T(8,128)(2,1)}) custom-call(s32[3]{0:T(128)} %get-tuple-element.43.place_ref, s32[32]{0:T(128)} %get-tuple-element.48.parent_ref, s32[32,2]{1,0:T(8,128)} %copy.27.map_ref, s32[32]{0:T(128)} %get-tuple-element.36.before_ref, f32[4,256,128]{2,1,0:T(8,128)} %get-tuple-element.14.base_ref, ...), custom_call_target="tpu_custom_call" | custom-call | tf_op jit(solution)/shard_map/factor_next/pallas_call | solution.py:123
  292.6 22.0 %exchange.4 = bf16[2,4,4,2,3,64,128]{6,5,4,3,2,1,0:T(8,128)(2,1)} custom-call(s32[1]{0:T(128)} %bitcast.25.root_ref, bf16[2,2,64,128]{3,2,1,0:T(8,128)(2,1)} %bitcast.68), custom_call_target="tpu_custom_call" | custom-call | tf_op jit(solution)/shard_map/exchange/pallas_call | solution.py:334
  314.6 23.7 %factor_next.4 = (f32[256,128]{1,0:T(8,128)}, bf16[256,128]{1,0:T(8,128)(2,1)}) custom-call(s32[3]{0:T(128)} %get-tuple-element.44.place_ref, s32[32]{0:T(128)} %get-tuple-element.47.parent_ref, s32[32,2]{1,0:T(8,128)} %copy.29.map_ref, s32[32]{0:T(128)} %get-tuple-element.37.before_ref, f32[4,256,128]{2,1,0:T(8,128)} %get-tuple-element.14.base_ref, ...), custom_call_target="tpu_custom_call" | custom-call | tf_op jit(solution)/shard_map/factor_next/pallas_call | solution.py:123
  338.4 22.9 %exchange.5 = bf16[2,4,4,2,3,64,128]{6,5,4,3,2,1,0:T(8,128)(2,1)} custom-call(s32[1]{0:T(128)} %bitcast.35.root_ref, bf16[2,2,64,128]{3,2,1,0:T(8,128)(2,1)} %bitcast.67), custom_call_target="tpu_custom_call" | custom-call | tf_op jit(solution)/shard_map/exchange/pallas_call | solution.py:334
  361.3 23.7 %factor_next.5 = (f32[256,128]{1,0:T(8,128)}, bf16[256,128]{1,0:T(8,128)(2,1)}) custom-call(s32[3]{0:T(128)} %get-tuple-element.45.place_ref, s32[32]{0:T(128)} %get-tuple-element.46.parent_ref, s32[32,2]{1,0:T(8,128)} %copy.30.map_ref, s32[32]{0:T(128)} %get-tuple-element.38.before_ref, f32[4,256,128]{2,1,0:T(8,128)} %get-tuple-element.14.base_ref, ...), custom_call_target="tpu_custom_call" | custom-call | tf_op jit(solution)/shard_map/factor_next/pallas_call | solution.py:123
  385.0 1.7 maximum_bitcast_fusion
  (16 shorter events, 0.0 us)
Async XLA Ops:
  6.5 3.3 copy-start.5
  6.5 7.8 %copy-start = (s32[4,32]{1,0:T(4,128)S(1)}, s32[4,32]{1,0:T(4,128)}, u32[]{:S(2)}) copy-start(s32[4,32]{1,0:T(4,128)} %param.13) | copy-start | bytes 1540
  6.5 12.5 %copy-start.6 = (s32[64,4,2]{0,2,1:T(2,128)S(1)}, s32[64,4,2]{0,2,1:T(2,128)}, u32[]{:S(2)}) copy-start(s32[64,4,2]{0,2,1:T(2,128)} %param.12) | copy-start | bytes 6148
  6.5 13.3 %copy-start.4 = (s32[64,4]{0,1:T(4,128)S(1)}, s32[64,4]{0,1:T(4,128)}, u32[]{:S(2)}) copy-start(s32[64,4]{0,1:T(4,128)} %param.11) | copy-start | bytes 3076
  6.5 89.8 %all-gather.3.cloned.1.call-start = ((), (), s32[]{:S(2)}) async-start(), calls=%async_computation | async-start | bytes 10485760 | tf_op jit(solution)/shard_map/all_gather | solution.py:356
  20.7 3.8 copy-start.7
  338.3 46.7 %copy-start.1 = (f32[256,128]{1,0:T(8,128)S(1)}, f32[256,128]{1,0:T(8,128)}, u32[]{:S(2)}) copy-start(f32[256,128]{1,0:T(8,128)} %get-tuple-element.16) | copy-start | bytes 393220
  338.3 46.7 %copy-start.2 = (f32[256,128]{1,0:T(8,128)S(1)}, f32[256,128]{1,0:T(8,128)}, u32[]{:S(2)}) copy-start(f32[256,128]{1,0:T(8,128)} %get-tuple-element.18) | copy-start | bytes 393220
  338.3 46.7 %copy-start.3 = (f32[256,128]{1,0:T(8,128)S(1)}, f32[256,128]{1,0:T(8,128)}, u32[]{:S(2)}) copy-start(f32[256,128]{1,0:T(8,128)} %get-tuple-element.20) | copy-start | bytes 393220
Sparse Core Ops, SparseCore 0:
  9.9 86.3 all-gather.2

commit v3 on v1

v3 whole, which is shorter than its diff:
```python
import functools

import jax
import jax.numpy as jnp
from jax import lax
from jax.experimental import pallas as pl
from jax.experimental.pallas import tpu as pltpu
from jax.sharding import PartitionSpec as P

F32 = jnp.float32
BF16 = jnp.bfloat16
B = 128
H = B // 2
WIRE = F32
TRANS_B = (((1,), (1,)), ((), ()))
TRANS_A = (((0,), (0,)), ((), ()))
MESH = pl.DeviceIdType.MESH
VMEM = pl.BlockSpec(memory_space=pltpu.VMEM)
SMEM = pl.BlockSpec(memory_space=pltpu.SMEM)
ANY = pl.BlockSpec(memory_space=pl.ANY)


def split_product(left, right):
    def parts(v):
        high = v.astype(BF16).astype(F32)
        mid = (v - high).astype(BF16).astype(F32)
        return high, mid, v - high - mid

    lh, lm, ll = parts(left)
    rh, rm, rl = parts(right)
    lefts = jnp.concatenate([lh, lh, lm, lh, ll, lm], axis=0).astype(BF16)
    rights = jnp.concatenate([rh, rm, rh, rl, rh, rm], axis=0).astype(BF16)
    return lax.dot_general(lefts, rights, TRANS_A, preferred_element_type=F32)


def cholesky_inverse(a):
    n = a.shape[0]
    lane = lax.broadcasted_iota(jnp.int32, (8, n), 1)
    sub = lax.broadcasted_iota(jnp.int32, (8, n), 0)
    upper, inverse = [], []
    next_a, rest_a, next_w, rest_w = a[:8], a[8:], None, None
    for j in range(n // 8):
        pa = next_a
        pw = (lane == sub + 8 * j).astype(F32)
        if next_w is not None:
            pw = pw + next_w
        cols = [jnp.broadcast_to(pa[:, 8 * j + t : 8 * j + t + 1], (8, n)) for t in range(8)]
        pivots = jnp.zeros((8, n), F32)
        for t in range(8):
            d = jnp.broadcast_to(cols[t][t : t + 1], (8, n))
            pivots = jnp.where(sub == t, d, pivots)
            if t < 7:
                ratio = jnp.where(sub > t, cols[t] * (1.0 / d), 0.0)
                for v in range(t + 1, 8):
                    cols[v] = cols[v] - ratio * cols[v][t : t + 1]
                pa = pa - ratio * pa[t : t + 1]
                pw = pw - ratio * pw[t : t + 1]
        scale = lax.rsqrt(pivots)
        scale = scale * (1.5 - 0.5 * pivots * scale * scale)
        pa = jnp.where(lane >= sub + 8 * j, pa * scale, 0.0)
        pw = pw * scale
        upper.append(pa)
        inverse.append(pw)
        if j + 1 < n // 8:
            both = jnp.concatenate([pa, pw], axis=1)
            first = split_product(pa[:, 8 * j + 8 : 8 * j + 16], both)
            next_a = rest_a[:8] - first[:, :n]
            next_w = -first[:, n:] if rest_w is None else rest_w[:8] - first[:, n:]
            if j + 2 < n // 8:
                step = split_product(pa[:, 8 * j + 16 :], both)
                rest_a = rest_a[8:] - step[:, :n]
                rest_w = -step[:, n:] if rest_w is None else rest_w[8:] - step[:, n:]
    return jnp.concatenate(upper, axis=0).T, jnp.concatenate(inverse, axis=0)


def products_kernel(step, live_ref, dest_ref, map_ref, panel_ref, head_ref, out_ref):
    live = live_ref[0]

    @pl.loop(0, out_ref.shape[0])
    def _(c):
        out_ref[c] = jnp.zeros(out_ref.shape[1:], F32)

    @pl.loop(0, (live + 3) // 4)
    def _(g):
        prods = []
        for u in range(4):
            i = g * 4 + u
            head = head_ref[i]
            head = jnp.where(i < live, head, jnp.zeros_like(head))
            prods.append(lax.dot_general(panel_ref[i], head, TRANS_B, preferred_element_type=F32))
        for u in range(4):
            i = g * 4 + u
            dest, first = dest_ref[i, step], map_ref[i, step * 2]
            out_ref[dest, pl.ds(pl.multiple_of(first * B, B), B), :] += prods[u][:B]
            out_ref[dest, pl.ds(pl.multiple_of(B - first * B, B), B), :] += prods[u][B:]


def slot_sums(step, live, dest, maps, panels, heads, col_count):
    src, rows, width = panels.shape
    return pl.pallas_call(
        functools.partial(products_kernel, step),
        out_shape=jax.ShapeDtypeStruct((col_count, rows, width), F32),
        in_specs=[SMEM, SMEM, SMEM, VMEM, VMEM],
        out_specs=VMEM,
        name="slot_sums",
    )(live, dest, maps, panels, heads.reshape(src, B, width))


def factor_kernel(step, parent_ref, map_ref, root_ref, base_ref, diag_ref, child_ref, *rest):
    out_ref, low_ref, upd, dg = rest[-4:]
    owner, row = lax.axis_index("col"), lax.axis_index("row")
    upd[...] = base_ref[...]
    dg[...] = diag_ref[...]
    if step:

        @pl.loop(0, parent_ref.shape[1])
        def _(k):
            @pl.when(parent_ref[step - 1, k] == owner)
            def _():
                parts = [child_ref[h, k, b] for b in range(3) for h in range(2)]
                head = jnp.concatenate(parts[4:], axis=0)
                prod = lax.dot_general(jnp.concatenate(parts[:4], axis=0), head, TRANS_B, preferred_element_type=F32)
                dg[...] -= lax.dot_general(head, head, TRANS_B, preferred_element_type=F32)
                first = map_ref[step - 1, k * 2]
                top = pl.multiple_of(first * B, B)
                low = pl.multiple_of(B - first * B, B)
                upd[pl.ds(low, B), :] -= prod[B:]

                @pl.when(root_ref[step - 1, k] != row)
                def _():
                    upd[pl.ds(top, B), :] -= prod[:B]

    lower, inverse = cholesky_inverse(dg[...])
    out_ref[...] = lax.dot_general(
        upd[...], inverse, TRANS_B, precision=lax.Precision.HIGHEST, preferred_element_type=F32
    )

    @pl.when(root_ref[step, owner] == row)
    def _():
        out_ref[:B] = lower

    low_ref[...] = out_ref[...].astype(BF16)


def factor(step, steps, parent, maps, roots, base, diag, child, panels):
    rows, width = base.shape
    whole = jax.ShapeDtypeStruct((steps, rows, width), F32)
    operands = [parent, maps, roots, base, diag, child] + ([panels] if step else [])
    return pl.pallas_call(
        functools.partial(factor_kernel, step),
        grid=(1,),
        out_shape=[whole, jax.ShapeDtypeStruct((rows, width), BF16)],
        in_specs=[SMEM, SMEM, SMEM, VMEM, VMEM, VMEM] + ([ANY] if step else []),
        out_specs=[pl.BlockSpec((None, rows, width), lambda i: (step, 0, 0)), VMEM],
        scratch_shapes=[pltpu.VMEM((rows, width), F32), pltpu.VMEM((B, width), F32)],
        input_output_aliases={6: 0} if step else {},
        name=f"factor_{step}",
    )(*operands)


def position():
    me = lax.axis_index("col")
    return me // 8, lax.rem(me // 2, 4), lax.rem(me, 2), lax.axis_index("row")


def at_x(d):
    x, y, p, _ = position()
    return lax.rem(x + d, 4), {"col": (lax.rem(x + d, 4) * 4 + y) * 2 + p}


def at_y(d):
    x, y, p, _ = position()
    return lax.rem(y + d, 4), {"col": (x * 4 + lax.rem(y + d, 4)) * 2 + p}


def at_z(d):
    return {"row": lax.rem(lax.axis_index("row") + d, 4)}


def partner():
    x, y, p, _ = position()
    return {"col": (x * 4 + y) * 2 + 1 - p}


def greet(peers):
    barrier = pltpu.get_barrier_semaphore()
    for peer in peers:
        pl.semaphore_signal(barrier, inc=1, device_id=peer, device_id_type=MESH)
    pl.semaphore_wait(barrier, len(peers))


class Copies:
    def __init__(self, send, recv):
        self.send, self.recv, self.all = send, recv, []

    def start(self, src, dst, peer):
        n = len(self.all)
        copy = pltpu.make_async_remote_copy(
            src_ref=src, dst_ref=dst, send_sem=self.send.at[n], recv_sem=self.recv.at[n], device_id=peer, device_id_type=MESH
        )
        copy.start()
        self.all.append(copy)
        return copy

    def finish(self):
        for copy in self.all:
            copy.wait_send()


class Broadcast:
    def __init__(self, copies, mine, out):
        row = lax.axis_index("row")
        self.copies, self.out = copies, out
        self.low, self.high = pl.ds(0, 8), pl.ds(8, 8)
        self.up = [copies.start(mine.at[part], out.at[row, part], at_z(1)) for part in (self.low, self.high)]
        self.down = [copies.start(mine.at[part], out.at[row, part], at_z(3)) for part in (self.high, self.low)]

    def relay(self):
        row = lax.axis_index("row")
        self.up[0].wait_recv()
        ref = self.out.at[lax.rem(row + 3, 4), self.low]
        self.on = [self.copies.start(ref, ref, at_z(1))]
        self.down[0].wait_recv()
        ref = self.out.at[lax.rem(row + 1, 4), self.high]
        self.on.append(self.copies.start(ref, ref, at_z(3)))

    def finish(self):
        for copy in [self.up[1], self.down[1]] + self.on:
            copy.wait_recv()


def open_kernel(dest_ref, root_ref, panels, out, chosen, zbuf, first, load_sem, send_sem, recv_sem):
    row = lax.axis_index("row")
    copies = Copies(send_sem, recv_sem)

    def quarter(q):
        return panels.at[pl.ds(q * 16, 16), pl.ds(0, B)]

    own = pltpu.make_async_copy(quarter(row), zbuf.at[row], load_sem)
    own.start()
    greet([at_z(d) for d in (1, 2, 3)])
    opened = [copies.start(quarter(lax.rem(row + d, 4)), zbuf.at[row], at_z(d)) for d in (2, 1, 3)]
    own.wait()
    for copy in opened:
        copy.wait_recv()
    steps = chosen.shape[0] + 1

    @pl.loop(0, 16)
    def _(j):
        first[j] = zbuf[root_ref[0, dest_ref[row * 16 + j, 0]], j]

    cast = Broadcast(copies, first, out)

    @pl.loop(0, 16)
    def _(j):
        out[row, j] = first[j]
        for s in range(1, steps):
            chosen[s - 1, j] = zbuf[root_ref[s, dest_ref[row * 16 + j, s]], j]

    cast.relay()
    cast.finish()
    copies.finish()


def open_heads(dest, roots, panels, steps):
    width = panels.shape[2]
    quarter = (16, B, width)
    return pl.pallas_call(
        open_kernel,
        out_shape=[jax.ShapeDtypeStruct((4,) + quarter, BF16), jax.ShapeDtypeStruct((steps - 1,) + quarter, BF16)],
        in_specs=[SMEM, SMEM, ANY],
        out_specs=[VMEM, VMEM],
        scratch_shapes=[
            pltpu.VMEM((4,) + quarter, BF16),
            pltpu.VMEM(quarter, BF16),
            pltpu.SemaphoreType.DMA,
            pltpu.SemaphoreType.DMA((9,)),
            pltpu.SemaphoreType.DMA((9,)),
        ],
        compiler_params=pltpu.CompilerParams(collective_id=0, has_side_effects=True),
        name="open_heads",
    )(dest, roots, panels)


class Exchange:
    rows, head = slice(0, 2), slice(2, 3)

    def __init__(self, copies, low, out, zbuf):
        self.copies, self.low, self.out, self.zbuf = copies, low, out, zbuf
        x, y, p, row = position()
        for h in range(2):
            out[h, x, y, p, :2] = low[:, h]
        zbuf[row] = low[1]

    def line(self, h, fixed, what):
        p = position()[2]
        return self.out.at[1, fixed, :, p, what] if h else self.out.at[0, :, fixed, p, what]

    def open_half(self, h, what, src):
        x, y, p, _ = position()
        move = at_y if h else at_x
        return [self.copies.start(src, self.out.at[h, x, y, p, what], move(d)[1]) for d in (2, 1, 3)]

    def begin(self):
        row = lax.axis_index("row")
        self.heads = [self.copies.start(self.low.at[1], self.zbuf.at[row], at_z(d)) for d in (2, 1, 3)]
        self.opened = [self.open_half(h, self.rows, self.low.at[:, h]) for h in range(2)]

    def pick(self, root):
        x, y, p, _ = position()
        for copy in self.heads:
            copy.wait_recv()
        picked = self.zbuf[root]
        for h in range(2):
            self.out[h, x, y, p, 2] = picked[h]
        self.opened_head = [self.open_half(h, self.head, self.out.at[h, x, y, p, self.head]) for h in range(2)]

    def turn_half(self, h, what, opened):
        x, y, _, _ = position()
        for copy in opened:
            copy.wait_recv()
        move, here = (at_x, x) if h else (at_y, y)
        ref = self.line(h, here, what)
        return [self.copies.start(ref, ref, move(d)[1]) for d in (2, 1, 3)], self.copies.start(ref, ref, partner())

    def turn(self):
        self.turned = [self.turn_half(h, self.rows, self.opened[h]) for h in range(2)]
        self.turned_head = [self.turn_half(h, self.head, self.opened_head[h]) for h in range(2)]

    def close_half(self, h, what, turned):
        self.done.append(turned[1])
        move = at_x if h else at_y
        for d, copy in zip((2, 1, 3), turned[0]):
            copy.wait_recv()
            ref = self.line(h, move(4 - d)[0], what)
            self.done.append(self.copies.start(ref, ref, partner()))

    def close(self):
        self.done = []
        for h in range(2):
            self.close_half(h, self.rows, self.turned[h])
        for h in range(2):
            self.close_half(h, self.head, self.turned_head[h])

    def finish(self):
        for copy in self.done:
            copy.wait_recv()


class Reduce:
    def __init__(self, copies, sums, target_ref, base_ref, refs):
        self.copies, self.sums, self.target_ref, self.base_ref = copies, sums, target_ref, base_ref
        self.acc, self.in0, self.wire, self.part, self.in1, self.in2, self.zbuf, load_sem = refs
        p = position()[2]
        self.load = pltpu.make_async_copy(sums.at[:, :, p], self.acc, load_sem)
        self.load.start()

    def begin(self):
        p = position()[2]
        self.first = self.copies.start(self.sums.at[:, :, 1 - p], self.in0, partner())

    def pair(self):
        self.load.wait()
        self.first.wait_recv()
        acc, in0, wire = self.acc, self.in0, self.wire

        @pl.loop(0, 16)
        def _(i):
            a, b = i // 4, lax.rem(i, 4)
            total = acc[a, b] + in0[a, b]
            acc[a, b] = total
            if WIRE != F32:
                wire[a, b] = total.astype(WIRE)

        src = acc if WIRE == F32 else wire
        self.second = []
        for d in (2, 1, 3):
            to, peer = at_x(d)
            self.second.append(self.copies.start(src.at[to, :, :B], self.in1.at[0, d - 1], peer))
            to, peer = at_y(d)
            self.second.append(self.copies.start(src.at[:, to, B:], self.in1.at[1, d - 1], peer))

    def cross(self):
        x, y, _, _ = position()
        for copy in self.second:
            copy.wait_recv()
        acc, in1, part = self.acc, self.in1, self.part

        @pl.loop(0, 4)
        def _(i):
            part[0, i] = acc[x, i, :B] + (in1[0, 0, i].astype(F32) + in1[0, 1, i].astype(F32) + in1[0, 2, i].astype(F32))
            part[1, i] = acc[i, y, B:] + (in1[1, 0, i].astype(F32) + in1[1, 1, i].astype(F32) + in1[1, 2, i].astype(F32))

        self.third = []
        for d in (2, 1, 3):
            to, peer = at_y(d)
            self.third.append(self.copies.start(part.at[0, to], self.in2.at[0, d - 1], peer))
            to, peer = at_x(d)
            self.third.append(self.copies.start(part.at[1, to], self.in2.at[1, d - 1], peer))

    def finish(self):
        x, y, _, row = position()
        for copy in self.third:
            copy.wait_recv()
        part, in2, zbuf = self.part, self.in2, self.zbuf
        base = self.target_ref[:B] - (part[0, y] + in2[0, 0] + in2[0, 1] + in2[0, 2])
        self.base_ref[:B] = base
        zbuf[row] = base
        self.fourth = [self.copies.start(zbuf.at[row], zbuf.at[row], at_z(d)) for d in (2, 1, 3)]
        self.base_ref[B:] = self.target_ref[B:] - (part[1, x] + in2[1, 0] + in2[1, 1] + in2[1, 2])

    def diagonal(self, diag_ref, root):
        for copy in self.fourth:
            copy.wait_recv()
        diag_ref[...] = self.zbuf[root]


def step_kernel(step, last, *refs):
    refs = list(refs)
    take = lambda n: [refs.pop(0) for _ in range(n)]
    root_ref, parent_ref, sums, target_ref = take(4)
    low = take(1)[0] if step else None
    mine = None if last else take(1)[0]
    base_ref, diag_ref = take(2)
    out = take(1)[0] if step else None
    heads = None if last else take(1)[0]
    reduce_refs = take(8)
    headbuf = take(1)[0] if step else None
    send_sem, recv_sem = refs
    me, row = lax.axis_index("col"), lax.axis_index("row")
    copies = Copies(send_sem, recv_sem)
    reduce = Reduce(copies, sums, target_ref.at[step], base_ref, reduce_refs)
    if step:
        exchange = Exchange(copies, low, out, headbuf)
    greet([partner()] + [at_z(d) for d in (1, 2, 3)] + [f(d)[1] for f in (at_x, at_y) for d in (1, 2, 3)])
    if step:
        exchange.begin()
    reduce.begin()
    if not last:
        cast = Broadcast(copies, mine.at[step], heads)
    if step:
        exchange.pick(root_ref[step, parent_ref[step - 1, me]])
    reduce.pair()
    if step:
        exchange.turn()
    if not last:
        heads[row] = mine[step]
        cast.relay()
    reduce.cross()
    if step:
        exchange.close()
    reduce.finish()
    if step:
        exchange.finish()
    if not last:
        cast.finish()
    reduce.diagonal(diag_ref, root_ref[step, me])
    copies.finish()


def step_exchange(step, steps, roots, parent, sums, targets, low, chosen):
    rows, width = targets.shape[1:]
    last = step == steps - 1
    operands = [roots, parent, sums.reshape(4, 4, 2, rows, width), targets]
    in_specs = [SMEM, SMEM, ANY, VMEM]
    outs = [jax.ShapeDtypeStruct((rows, width), F32), jax.ShapeDtypeStruct((B, width), F32)]
    scratch = [
        pltpu.VMEM((4, 4, rows, width), F32),
        pltpu.VMEM((4, 4, rows, width), F32),
        pltpu.VMEM((4, 4, rows, width) if WIRE != F32 else (1, 1, 8, width), WIRE),
        pltpu.VMEM((2, 4, B, width), F32),
        pltpu.VMEM((2, 3, 4, B, width), WIRE),
        pltpu.VMEM((2, 3, B, width), F32),
        pltpu.VMEM((4, B, width), F32),
        pltpu.SemaphoreType.DMA,
    ]
    count = 16
    if step:
        operands.append(low.reshape(2, 2, H, width))
        in_specs.append(VMEM)
        outs.append(jax.ShapeDtypeStruct((2, 4, 4, 2, 3, H, width), BF16))
        scratch.append(pltpu.VMEM((4, 2, H, width), BF16))
        count += 43
    if not last:
        operands.append(chosen)
        in_specs.append(VMEM)
        outs.append(jax.ShapeDtypeStruct((4, 16, B, width), BF16))
        count += 6
    got = pl.pallas_call(
        functools.partial(step_kernel, step, last),
        out_shape=outs,
        in_specs=in_specs,
        out_specs=[VMEM] * len(outs),
        scratch_shapes=scratch + [pltpu.SemaphoreType.DMA((count,)), pltpu.SemaphoreType.DMA((count,))],
        compiler_params=pltpu.CompilerParams(collective_id=1 + step, has_side_effects=True),
        name=f"step_{step}",
    )(*operands)
    base, diag = got[:2]
    child = got[2].reshape(2, 32, 3, H, width) if step else jnp.zeros((2, 1, 3, 8, width), BF16)
    return base, diag, child, None if last else got[-1]


def local(targets, src_panels, live_counts, dest_owner, relative_map, diag_row, parent, chain_map):
    cols = lax.axis_size("col")
    steps, src = targets.shape[0], src_panels.shape[0]
    maps = relative_map.reshape(src, -1)
    chains = chain_map.reshape(steps - 1, -1)
    heads, chosen = open_heads(dest_owner, diag_row, src_panels, steps)
    out = low = None
    for s in range(steps):
        sums = slot_sums(s, live_counts, dest_owner, maps, src_panels, heads, cols)
        base, diag, child, heads = step_exchange(s, steps, diag_row, parent, sums, targets[:, 0], low, chosen)
        out, low = factor(s, steps, parent, chains, diag_row, base, diag, child, out)
    return out[:, None]


def solution(mesh):
    return jax.shard_map(
        local,
        mesh=mesh,
        in_specs=(
            P(None, "col", "row", None),
            P("col", "row", None),
            P("col"),
            P("col", None),
            P("col", None, "row"),
            P(),
            P(),
            P(None, None, "row"),
        ),
        out_specs=P(None, "col", "row", None),
        check_vma=False,
    )
```

time: 792 us -> 293 us (0.37)
  waiting for transfers between devices: 521 us -> 0 us
  Pallas kernels: 127 us -> 287 us
  blocking collectives: 67.6 us -> 0 us
  between operations: 35.3 us -> 0.7 us
  local copies, waits for them, and re-layouts: 29.7 us -> 4.83 us
  other arithmetic: 9.7 us -> 0 us
    reduce_scatter x4 -> x0, waiting for transfers between devices: 340 us -> none  [local(): got = lax.psum_scatter(sums[s], 'col', scatter_dimension=0, tiled=False)]
    all_gather x4 -> x0, waiting for transfers between devices: 180 us -> none  [the longest x3 98.7 us: local(): child = lax.all_gather(jnp.concatenate([low, head], axis=0), 'col', axis=0)]
    pallas_call x5 -> x13, Pallas kernels: 127 us -> 287 us  [the longest x4 159 us: step_exchange(): pl.pallas_call(functools.partial(step_kernel, step, last), out_shape=outs...]
    all_gather x7 -> x0, blocking collectives: 67.6 us -> none  [the longest x4 38.7 us: local(): diags.append(lax.all_gather(base[:B], 'row', axis=0)[diag_row[s, owner]])]
    squeeze x13 -> x0, local copies, waits for them, and re-layouts: 17.4 us -> none  [the longest x1 12.2 us: local(): got = lax.psum_scatter(sums[s], 'col', scatter_dimension=0, tiled=False)]
  transfers between devices with their start and end apart: 8 -> 0, of which waited for: 8 -> 0; matrix products, arithmetic and copies ran while one was open for 2% -> 0% of each run, Pallas kernels for 0% -> 0%
where the time goes in v3:
time: 293 us; the launch traced here: 292 us
  Pallas kernels  287 us (98%)
  local copies, waits for them, and re-layouts  4.83 us (2%)
    pallas_call x4, Pallas kernels, step_exchange(): pl.pallas_call(functools.partial(step_kernel, step, last), out_shape=outs...  159 us
    pallas_call x1, Pallas kernels, open_heads(): pl.pallas_call(open_kernel, out_shape=[jax.ShapeDtypeStruct((4,) + quarte...  51.4 us
    pallas_call x4, Pallas kernels, factor(): pl.pallas_call(functools.partial(factor_kernel, step), grid=(1,), out_sha...  39.1 us
    pallas_call x4, Pallas kernels, slot_sums(): pl.pallas_call(functools.partial(products_kernel, step), out_shape=jax.Sh...  36.8 us

profile of v3, /device:TPU:1, one launch (start us, length us, event | category | flops | bytes accessed | tf_op | source)
XLA Modules:
  0.0 292.0 jit_solution(15156507547290386822)
XLA Ops:
  0.7 1.4 copy.28.dest_ref
  2.0 1.4 copy.29.map_ref
  3.4 0.8 copy.20
  4.2 0.7 reshape.48.map_ref
  4.9 51.4 %open_heads.1 = (bf16[4,16,128,128]{3,2,1,0:T(8,128)(2,1)}, bf16[3,16,128,128]{3,2,1,0:T(8,128)(2,1)}) custom-call(s32[64,4]{1,0:T(8,128)} %copy.28.dest_ref, s32[4,32]{1,0:T(4,128)} %root_ref.9, bf16[64,256,128]{2,1,0:T(8,128)(2,1)} %panel_ref.7), custom_call_target="tpu_custom_call" | custom-call | tf_op jit(solution)/shard_map/open_heads/pallas_call | solution.py:268
  56.3 9.1 %slot_sums.4 = f32[32,256,128]{2,1,0:T(8,128)} custom-call(s32[1]{0:T(128)S(6)} %copy.34.live_ref, s32[64,4]{1,0:T(8,128)} %copy.28.dest_ref, s32[64,8]{1,0:T(8,128)} %copy.29.map_ref, bf16[64,256,128]{2,1,0:T(8,128)(2,1)} %panel_ref.7, bf16[64,128,128]{2,1,0:T(8,128)(2,1)} %bitcast.33), custom_call_target="tpu_custom_call" | custom-call | tf_op jit(solution)/shard_map/slot_sums/pallas_call | solution.py:100
  65.4 33.4 %step_0.1 = (f32[256,128]{1,0:T(8,128)}, f32[128,128]{1,0:T(8,128)}, bf16[4,16,128,128]{3,2,1,0:T(8,128)(2,1)}) custom-call(s32[4,32]{1,0:T(4,128)} %root_ref.9, s32[3,32]{1,0:T(4,128)} %parent_ref.7, f32[4,4,2,256,128]{4,3,2,1,0:T(8,128)} %bitcast.22, f32[4,256,128]{2,1,0:T(8,128)} %bitcast.23, bf16[3,16,128,128]{3,2,1,0:T(8,128)(2,1)} %get-tuple-element.29.refs_4_.refs_5_), custom_call_target="tpu_custom_call" | custom-call | tf_op jit(solution)/shard_map/step_0/pallas_call | solution.py:489
  98.8 0.6 broadcast_in_dim.6.child_ref
  99.4 8.4 %factor_0.1 = (f32[4,256,128]{2,1,0:T(8,128)}, bf16[256,128]{1,0:T(8,128)(2,1)}) custom-call(s32[3,32]{1,0:T(4,128)} %parent_ref.7, s32[3,64]{1,0:T(4,128)} %reshape.48.map_ref, s32[4,32]{1,0:T(4,128)} %root_ref.9, f32[256,128]{1,0:T(8,128)} %get-tuple-element.31.base_ref, f32[128,128]{1,0:T(8,128)} %get-tuple-element.32.diag_ref, ...), custom_call_target="tpu_custom_call" | custom-call | tf_op jit(solution)/shard_map/factor_0/pallas_call | solution.py:149
  107.9 9.1 %slot_sums.5 = f32[32,256,128]{2,1,0:T(8,128)} custom-call(s32[1]{0:T(128)S(6)} %copy.34.live_ref, s32[64,4]{1,0:T(8,128)} %copy.28.dest_ref, s32[64,8]{1,0:T(8,128)} %copy.29.map_ref, bf16[64,256,128]{2,1,0:T(8,128)(2,1)} %panel_ref.7, bf16[64,128,128]{2,1,0:T(8,128)(2,1)} %bitcast.31), custom_call_target="tpu_custom_call" | custom-call | tf_op jit(solution)/shard_map/slot_sums/pallas_call | solution.py:100
  117.0 43.2 %step_1.1 = (f32[256,128]{1,0:T(8,128)}, f32[128,128]{1,0:T(8,128)}, bf16[2,4,4,2,3,64,128]{6,5,4,3,2,1,0:T(8,128)(2,1)}, bf16[4,16,128,128]{3,2,1,0:T(8,128)(2,1)}) custom-call(s32[4,32]{1,0:T(4,128)} %root_ref.9, s32[3,32]{1,0:T(4,128)} %parent_ref.7, f32[4,4,2,256,128]{4,3,2,1,0:T(8,128)} %bitcast.21, f32[4,256,128]{2,1,0:T(8,128)} %bitcast.24, ...), custom_call_target="tpu_custom_call" | custom-call | tf_op jit(solution)/shard_map/step_1/pallas_call | solution.py:489
  160.2 10.3 %factor_1.1 = (f32[4,256,128]{2,1,0:T(8,128)}, bf16[256,128]{1,0:T(8,128)(2,1)}) custom-call(s32[3,32]{1,0:T(4,128)} %parent_ref.7, s32[3,64]{1,0:T(4,128)} %reshape.48.map_ref, s32[4,32]{1,0:T(4,128)} %root_ref.9, f32[256,128]{1,0:T(8,128)} %get-tuple-element.35.base_ref, f32[128,128]{1,0:T(8,128)} %get-tuple-element.36.diag_ref, ...), custom_call_target="tpu_custom_call", output_to_operand_aliasing={{0}: (6, {})} | custom-call | tf_op jit(solution)/shard_map/factor_1/pallas_call | solution.py:149
  170.6 9.1 %slot_sums.6 = f32[32,256,128]{2,1,0:T(8,128)} custom-call(s32[1]{0:T(128)S(6)} %copy.34.live_ref, s32[64,4]{1,0:T(8,128)} %copy.28.dest_ref, s32[64,8]{1,0:T(8,128)} %copy.29.map_ref, bf16[64,256,128]{2,1,0:T(8,128)(2,1)} %panel_ref.7, bf16[64,128,128]{2,1,0:T(8,128)(2,1)} %bitcast.32), custom_call_target="tpu_custom_call" | custom-call | tf_op jit(solution)/shard_map/slot_sums/pallas_call | solution.py:100
  179.7 42.4 %step_2.1 = (f32[256,128]{1,0:T(8,128)}, f32[128,128]{1,0:T(8,128)}, bf16[2,4,4,2,3,64,128]{6,5,4,3,2,1,0:T(8,128)(2,1)}, bf16[4,16,128,128]{3,2,1,0:T(8,128)(2,1)}) custom-call(s32[4,32]{1,0:T(4,128)} %root_ref.9, s32[3,32]{1,0:T(4,128)} %parent_ref.7, f32[4,4,2,256,128]{4,3,2,1,0:T(8,128)} %bitcast.20, f32[4,256,128]{2,1,0:T(8,128)} %bitcast.25, ...), custom_call_target="tpu_custom_call" | custom-call | tf_op jit(solution)/shard_map/step_2/pallas_call | solution.py:489
  222.2 10.1 %factor_2.1 = (f32[4,256,128]{2,1,0:T(8,128)}, bf16[256,128]{1,0:T(8,128)(2,1)}) custom-call(s32[3,32]{1,0:T(4,128)} %parent_ref.7, s32[3,64]{1,0:T(4,128)} %reshape.48.map_ref, s32[4,32]{1,0:T(4,128)} %root_ref.9, f32[256,128]{1,0:T(8,128)} %get-tuple-element.41.base_ref, f32[128,128]{1,0:T(8,128)} %get-tuple-element.42.diag_ref, ...), custom_call_target="tpu_custom_call", output_to_operand_aliasing={{0}: (6, {})} | custom-call | tf_op jit(solution)/shard_map/factor_2/pallas_call | solution.py:149
  232.2 9.3 %slot_sums.7 = f32[32,256,128]{2,1,0:T(8,128)} custom-call(s32[1]{0:T(128)S(6)} %copy.34.live_ref, s32[64,4]{1,0:T(8,128)} %copy.28.dest_ref, s32[64,8]{1,0:T(8,128)} %copy.29.map_ref, bf16[64,256,128]{2,1,0:T(8,128)(2,1)} %panel_ref.7, bf16[64,128,128]{2,1,0:T(8,128)(2,1)} %bitcast.30), custom_call_target="tpu_custom_call" | custom-call | tf_op jit(solution)/shard_map/slot_sums/pallas_call | solution.py:100
  241.6 40.2 %step_3.1 = (f32[256,128]{1,0:T(8,128)}, f32[128,128]{1,0:T(8,128)}, bf16[2,4,4,2,3,64,128]{6,5,4,3,2,1,0:T(8,128)(2,1)}) custom-call(s32[4,32]{1,0:T(4,128)} %root_ref.9, s32[3,32]{1,0:T(4,128)} %parent_ref.7, f32[4,4,2,256,128]{4,3,2,1,0:T(8,128)} %bitcast.19, f32[4,256,128]{2,1,0:T(8,128)} %bitcast.26, bf16[2,2,64,128]{3,2,1,0:T(8,128)(2,1)} %bitcast.34), custom_call_target="tpu_custom_call" | custom-call | tf_op jit(solution)/shard_map/step_3/pallas_call | solution.py:489
  281.8 10.2 %factor_3.1 = (f32[4,256,128]{2,1,0:T(8,128)}, bf16[256,128]{1,0:T(8,128)(2,1)}) custom-call(s32[3,32]{1,0:T(4,128)} %parent_ref.7, s32[3,64]{1,0:T(4,128)} %reshape.48.map_ref, s32[4,32]{1,0:T(4,128)} %root_ref.9, f32[256,128]{1,0:T(8,128)} %get-tuple-element.46.base_ref, f32[128,128]{1,0:T(8,128)} %get-tuple-element.47.diag_ref, ...), custom_call_target="tpu_custom_call", output_to_operand_aliasing={{0}: (6, {})} | custom-call | tf_op jit(solution)/shard_map/factor_3/pallas_call | solution.py:149

commit v4 on v3

v4 whole, which is shorter than its diff:
```python
import functools

import jax
import jax.numpy as jnp
from jax import lax
from jax.experimental import pallas as pl
from jax.experimental.pallas import tpu as pltpu
from jax.sharding import PartitionSpec as P

F32 = jnp.float32
BF16 = jnp.bfloat16
B = 128
H = B // 2
TRANS_B = (((1,), (1,)), ((), ()))
TRANS_A = (((0,), (0,)), ((), ()))
MESH = pl.DeviceIdType.MESH
VMEM = pl.BlockSpec(memory_space=pltpu.VMEM)
SMEM = pl.BlockSpec(memory_space=pltpu.SMEM)
ANY = pl.BlockSpec(memory_space=pl.ANY)


def split_product(left, right):
    def parts(v):
        high = v.astype(BF16).astype(F32)
        mid = (v - high).astype(BF16).astype(F32)
        return high, mid, v - high - mid

    lh, lm, ll = parts(left)
    rh, rm, rl = parts(right)
    lefts = jnp.concatenate([lh, lh, lm, lh, ll, lm], axis=0).astype(BF16)
    rights = jnp.concatenate([rh, rm, rh, rl, rh, rm], axis=0).astype(BF16)
    return lax.dot_general(lefts, rights, TRANS_A, preferred_element_type=F32)


def cholesky_inverse(a, midway=None):
    n = a.shape[0]
    lane = lax.broadcasted_iota(jnp.int32, (8, n), 1)
    sub = lax.broadcasted_iota(jnp.int32, (8, n), 0)
    upper, inverse = [], []
    next_a, rest_a, next_w, rest_w = a[:8], a[8:], None, None
    for j in range(n // 8):
        if j == 10 and midway is not None:
            midway()
        pa = next_a
        pw = (lane == sub + 8 * j).astype(F32)
        if next_w is not None:
            pw = pw + next_w
        cols = [jnp.broadcast_to(pa[:, 8 * j + t : 8 * j + t + 1], (8, n)) for t in range(8)]
        pivots = jnp.zeros((8, n), F32)
        for t in range(8):
            d = jnp.broadcast_to(cols[t][t : t + 1], (8, n))
            pivots = jnp.where(sub == t, d, pivots)
            if t < 7:
                ratio = jnp.where(sub > t, cols[t] * (1.0 / d), 0.0)
                for v in range(t + 1, 8):
                    cols[v] = cols[v] - ratio * cols[v][t : t + 1]
                pa = pa - ratio * pa[t : t + 1]
                pw = pw - ratio * pw[t : t + 1]
        scale = lax.rsqrt(pivots)
        scale = scale * (1.5 - 0.5 * pivots * scale * scale)
        pa = jnp.where(lane >= sub + 8 * j, pa * scale, 0.0)
        pw = pw * scale
        upper.append(pa)
        inverse.append(pw)
        if j + 1 < n // 8:
            both = jnp.concatenate([pa, pw], axis=1)
            first = split_product(pa[:, 8 * j + 8 : 8 * j + 16], both)
            next_a = rest_a[:8] - first[:, :n]
            next_w = -first[:, n:] if rest_w is None else rest_w[:8] - first[:, n:]
            if j + 2 < n // 8:
                step = split_product(pa[:, 8 * j + 16 :], both)
                rest_a = rest_a[8:] - step[:, :n]
                rest_w = -step[:, n:] if rest_w is None else rest_w[8:] - step[:, n:]
    return jnp.concatenate(upper, axis=0).T, jnp.concatenate(inverse, axis=0)


def position():
    me = lax.axis_index("col")
    return me // 8, lax.rem(me // 2, 4), lax.rem(me, 2), lax.axis_index("row")


def at_x(d):
    x, y, p, _ = position()
    return lax.rem(x + d, 4), {"col": (lax.rem(x + d, 4) * 4 + y) * 2 + p}


def at_y(d):
    x, y, p, _ = position()
    return lax.rem(y + d, 4), {"col": (x * 4 + lax.rem(y + d, 4)) * 2 + p}


def at_z(d):
    return {"row": lax.rem(lax.axis_index("row") + d, 4)}


def partner():
    x, y, p, _ = position()
    return {"col": (x * 4 + y) * 2 + 1 - p}


def greet(peers):
    barrier = pltpu.get_barrier_semaphore()
    for peer in peers:
        pl.semaphore_signal(barrier, inc=1, device_id=peer, device_id_type=MESH)
    pl.semaphore_wait(barrier, len(peers))


class Copies:
    def __init__(self, send, recv):
        self.send, self.recv, self.count, self.open = send, recv, 0, []

    def start(self, src, dst, peer):
        n = self.count
        copy = pltpu.make_async_remote_copy(
            src_ref=src, dst_ref=dst, send_sem=self.send.at[n], recv_sem=self.recv.at[n], device_id=peer, device_id_type=MESH
        )
        copy.start()
        self.count += 1
        self.open.append(copy)
        return copy

    def sent(self, copies):
        for copy in copies:
            copy.wait_send()
        self.open = [copy for copy in self.open if all(copy is not other for other in copies)]

    def finish(self):
        self.sent(self.open)


class Broadcast:
    def __init__(self, copies, mine, out):
        row = lax.axis_index("row")
        self.copies, self.out = copies, out
        self.low, self.high = pl.ds(0, 8), pl.ds(8, 8)
        self.up = [copies.start(mine.at[part], out.at[row, part], at_z(1)) for part in (self.low, self.high)]
        self.down = [copies.start(mine.at[part], out.at[row, part], at_z(3)) for part in (self.high, self.low)]

    def relay(self):
        row = lax.axis_index("row")
        self.up[0].wait_recv()
        ref = self.out.at[lax.rem(row + 3, 4), self.low]
        self.on = [self.copies.start(ref, ref, at_z(1))]
        self.down[0].wait_recv()
        ref = self.out.at[lax.rem(row + 1, 4), self.high]
        self.on.append(self.copies.start(ref, ref, at_z(3)))

    def finish(self):
        for copy in [self.up[1], self.down[1]] + self.on:
            copy.wait_recv()


class Exchange:
    rows, head = slice(0, 2), slice(2, 3)

    def __init__(self, copies, low, out, zbuf):
        self.copies, self.out, self.zbuf = copies, out, zbuf
        x, y, p, row = position()
        for h in range(2):
            zbuf[row, h] = low[B + h * H : B + (h + 1) * H]
        for h in range(2):
            for b in range(2):
                out[h, x, y, p, b] = low[b * B + h * H : b * B + (h + 1) * H]

    def line(self, h, fixed, what):
        p = position()[2]
        return self.out.at[1, fixed, :, p, what] if h else self.out.at[0, :, fixed, p, what]

    def open_half(self, h, what, src):
        x, y, p, _ = position()
        move = at_y if h else at_x
        return [self.copies.start(src, self.out.at[h, x, y, p, what], move(d)[1]) for d in (2, 1, 3)]

    def begin(self):
        x, y, p, row = position()
        self.heads = [self.copies.start(self.zbuf.at[row], self.zbuf.at[row], at_z(d)) for d in (2, 1, 3)]
        self.opened = [self.open_half(h, self.rows, self.out.at[h, x, y, p, self.rows]) for h in range(2)]

    def pick(self, root):
        x, y, p, _ = position()
        for copy in self.heads:
            copy.wait_recv()
        picked = self.zbuf[root]
        for h in range(2):
            self.out[h, x, y, p, 2] = picked[h]
        self.opened_head = [self.open_half(h, self.head, self.out.at[h, x, y, p, self.head]) for h in range(2)]

    def turn_half(self, h, what, opened):
        x, y, _, _ = position()
        for copy in opened:
            copy.wait_recv()
        move, here = (at_x, x) if h else (at_y, y)
        ref = self.line(h, here, what)
        return [self.copies.start(ref, ref, move(d)[1]) for d in (2, 1, 3)], self.copies.start(ref, ref, partner())

    def turn(self):
        self.turned = [self.turn_half(h, self.rows, self.opened[h]) for h in range(2)]
        self.turned_head = [self.turn_half(h, self.head, self.opened_head[h]) for h in range(2)]

    def close_half(self, h, what, turned):
        self.done.append(turned[1])
        move = at_x if h else at_y
        for d, copy in zip((2, 1, 3), turned[0]):
            copy.wait_recv()
            ref = self.line(h, move(4 - d)[0], what)
            self.done.append(self.copies.start(ref, ref, partner()))

    def close(self):
        self.done = []
        for h in range(2):
            self.close_half(h, self.rows, self.turned[h])
        for h in range(2):
            self.close_half(h, self.head, self.turned_head[h])

    def finish(self):
        for copy in self.done:
            copy.wait_recv()


class Reduce:
    def __init__(self, copies, acc, away, in0, part, in1, in2, zbuf):
        self.copies, self.acc, self.away = copies, acc, away
        self.in0, self.part, self.in1, self.in2, self.zbuf = in0, part, in1, in2, zbuf

    def begin(self, previous, sums, slot):
        p = position()[2]
        if previous is not None:
            self.copies.sent([previous.first])
        self.own = lambda i: sums[slot(i * 2 + p)]

        @pl.loop(0, 16)
        def _(i):
            self.away[i // 4, lax.rem(i, 4)] = sums[slot(i * 2 + 1 - p)]

        self.first = self.copies.start(self.away, self.in0, partner())

    def pair(self, previous):
        if previous is not None:
            self.copies.sent(previous.second)
        self.first.wait_recv()
        acc, in0 = self.acc, self.in0

        @pl.loop(0, 16)
        def _(i):
            acc[i // 4, lax.rem(i, 4)] = self.own(i) + in0[i // 4, lax.rem(i, 4)]

        self.second = []
        for d in (2, 1, 3):
            to, peer = at_x(d)
            self.second.append(self.copies.start(acc.at[to, :, :B], self.in1.at[0, d - 1], peer))
            to, peer = at_y(d)
            self.second.append(self.copies.start(acc.at[:, to, B:], self.in1.at[1, d - 1], peer))

    def cross(self):
        x, y, _, _ = position()
        for copy in self.second:
            copy.wait_recv()
        acc, in1, part = self.acc, self.in1, self.part

        @pl.loop(0, 4)
        def _(i):
            part[0, i] = acc[x, i, :B] + (in1[0, 0, i] + in1[0, 1, i] + in1[0, 2, i])
            part[1, i] = acc[i, y, B:] + (in1[1, 0, i] + in1[1, 1, i] + in1[1, 2, i])

        self.third = []
        for d in (2, 1, 3):
            to, peer = at_y(d)
            self.third.append(self.copies.start(part.at[0, to], self.in2.at[0, d - 1], peer))
            to, peer = at_x(d)
            self.third.append(self.copies.start(part.at[1, to], self.in2.at[1, d - 1], peer))

    def finish(self, target, base):
        x, y, _, row = position()
        for copy in self.third:
            copy.wait_recv()
        part, in2, zbuf = self.part, self.in2, self.zbuf
        top = target[:B] - (part[0, y] + in2[0, 0] + in2[0, 1] + in2[0, 2])
        zbuf[row] = top
        base[:B] = top
        base[B:] = target[B:] - (part[1, x] + in2[1, 0] + in2[1, 1] + in2[1, 2])
        self.fourth = [self.copies.start(zbuf.at[row], zbuf.at[row], at_z(d)) for d in (2, 1, 3)]

    def diagonal(self, root):
        for copy in self.fourth:
            copy.wait_recv()
        return self.zbuf[root]


def window_kernel(
    dest_ref, map_ref, pred_ref, last_ref, root_ref, parent_ref, chain_ref, panel_hbm, target_ref, out_ref,
    panels, zb, chosen, heads, sums, away, acc, in0, part, in1, in2, upd, load_sem, send_sem, recv_sem, *bufs,
):
    steps = target_ref.shape[0]
    diags, child, headbuf = bufs[:steps], bufs[steps : 2 * steps - 1], bufs[2 * steps - 1 :]
    src = panels.shape[0]
    x, y, p, row = position()
    me = lax.axis_index("col")
    copies = Copies(send_sem, recv_sem)
    load = pltpu.make_async_copy(panel_hbm, panels, load_sem.at[0])

    def quarter(q):
        return panel_hbm.at[pl.ds(q * 16, 16), 0]

    own = pltpu.make_async_copy(quarter(row), zb.at[row], load_sem.at[1])
    own.start()
    sums[src] = jnp.zeros(sums.shape[1:], F32)
    greet([partner()] + [at_z(d) for d in (1, 2, 3)] + [f(d)[1] for f in (at_x, at_y) for d in (1, 2, 3)])
    opened = [copies.start(quarter(lax.rem(row + d, 4)), zb.at[row], at_z(d)) for d in (2, 1, 3)]
    load.start()
    own.wait()
    for copy in opened:
        copy.wait_recv()

    def choose(s):
        @pl.loop(0, 16)
        def _(j):
            chosen[s, j] = zb[root_ref[s, dest_ref[s, row * 16 + j]], j]

    def keep(s):
        @pl.loop(0, 16)
        def _(j):
            heads[s, row, j] = chosen[s, j]

    def products(s, quarters):
        @pl.loop(quarters[0] * 4, quarters[1] * 4)
        def _(g):
            prods = []
            for u in range(4):
                i = g * 4 + u
                first = map_ref[s, 0, i]
                block = jnp.concatenate([panels[i, first], panels[i, 1 - first]], axis=0)
                prods.append(
                    lax.dot_general(block, heads[s, i // 16, lax.rem(i, 16)], TRANS_B, preferred_element_type=F32)
                )
            for u in range(4):
                i = g * 4 + u
                sums[i] = prods[u] + sums[pred_ref[s, i]]

    reduces = [
        Reduce(copies, acc, away, in0.at[s], part.at[s], in1.at[s], in2.at[s], diags[s]) for s in range(steps)
    ]
    casts = {}

    def cast(s):
        casts[s] = Broadcast(copies, chosen.at[s], heads.at[s])

    def begin(s):
        reduces[s].begin(reduces[s - 1] if s else None, sums, lambda c: last_ref[s, c])

    def factor(s, midway):
        diag = reduces[s].diagonal(root_ref[s, me])
        upd[s, 2 * B :] = diag
        if s:

            @pl.loop(0, 16)
            def _(g):
                lefts, rights = [], []
                for u in range(2):
                    k = g * 2 + u
                    a, b, c = k // 8, lax.rem(k // 2, 4), u
                    chosen_child = parent_ref[s - 1, k] == me
                    head = jnp.concatenate([child[s - 1][h, a, b, c, 2] for h in range(2)], axis=0)
                    head = jnp.where(chosen_child, head, jnp.zeros_like(head))
                    first = chain_ref[s - 1, 0, k]
                    left_out = root_ref[s - 1, k] == row
                    blocks = []
                    for q in (first, 1 - first):
                        block = jnp.concatenate([child[s - 1][h, a, b, c, q] for h in range(2)], axis=0)
                        blocks.append(jnp.where(left_out & (q == 0), jnp.zeros_like(block), block))
                    lefts.append(jnp.concatenate(blocks + [head], axis=0))
                    rights.append(head)
                upd[s] -= lax.dot_general(
                    jnp.concatenate(lefts, axis=1), jnp.concatenate(rights, axis=1), TRANS_B, preferred_element_type=F32
                )

        lower, inverse = cholesky_inverse(upd[s, 2 * B :], midway)
        solved = lax.dot_general(
            upd[s, : 2 * B], inverse, TRANS_B, precision=lax.Precision.HIGHEST, preferred_element_type=F32
        )
        top = jnp.where(root_ref[s, me] == row, lower, solved[:B])
        panel = jnp.concatenate([top, solved[B:]], axis=0)
        out_ref[s] = panel
        return panel.astype(BF16)

    choose(0)
    cast(0)
    keep(0)
    for s in range(1, steps):
        choose(s)
        keep(s)
    casts[0].relay()
    cast(1)
    load.wait()
    casts[0].finish()
    products(0, (0, 4))
    begin(0)
    casts[1].relay()
    reduces[0].pair(None)
    casts[1].finish()
    products(1, (0, 4))
    begin(1)
    reduces[0].cross()
    reduces[1].pair(reduces[0])
    reduces[0].finish(target_ref.at[0], upd.at[0, : 2 * B])
    cast(2)
    low = factor(0, casts[2].relay)
    for s in range(steps - 1):
        ahead = s + 2 if s + 2 < steps else None
        exchange = Exchange(copies, low, child[s], headbuf[s])
        exchange.begin()
        reduces[s + 1].cross()
        exchange.pick(root_ref[s + 1, parent_ref[s, me]])
        if ahead:
            casts[ahead].finish()
            products(ahead, (0, 2))
        exchange.turn()
        if ahead:
            products(ahead, (2, 4))
            begin(ahead)
        reduces[s + 1].finish(target_ref.at[s + 1], upd.at[s + 1, : 2 * B])
        exchange.close()
        midway = None
        if s + 3 < steps:
            cast(s + 3)
            midway = casts[s + 3].relay
        if ahead:
            reduces[ahead].pair(reduces[ahead - 1])
        exchange.finish()
        low = factor(s + 1, midway)
    copies.finish()


def local(targets, src_panels, live_counts, dest_owner, relative_map, diag_row, parent, chain_map):
    steps, _, rows, width = targets.shape
    src = src_panels.shape[0]
    cols = lax.axis_size("col")
    dest = dest_owner.T
    index = jnp.arange(src)
    before = (dest[:, :, None] == dest[:, None, :]) & (index[None, :] < index[:, None])
    pred = jnp.max(jnp.where(before, index, -1), axis=2)
    pred = jnp.where(pred < 0, src, pred).astype(jnp.int32)
    mine = (dest[:, None, :] == jnp.arange(cols)[:, None]) & (index < live_counts[0])
    last = jnp.max(jnp.where(mine, index, -1), axis=2)
    last = jnp.where(last < 0, src, last).astype(jnp.int32)
    copies = 3 + steps * 22 + (steps - 1) * 43
    out = pl.pallas_call(
        window_kernel,
        out_shape=jax.ShapeDtypeStruct((steps, rows, width), F32),
        in_specs=[SMEM] * 7 + [ANY, VMEM],
        out_specs=VMEM,
        scratch_shapes=[
            pltpu.VMEM((src, 2, B, width), BF16),
            pltpu.VMEM((4, 16, B, width), BF16),
            pltpu.VMEM((steps, 16, B, width), BF16),
            pltpu.VMEM((steps, 4, 16, B, width), BF16),
            pltpu.VMEM((src + 1, rows, width), F32),
            pltpu.VMEM((4, 4, rows, width), F32),
            pltpu.VMEM((4, 4, rows, width), F32),
            pltpu.VMEM((steps, 4, 4, rows, width), F32),
            pltpu.VMEM((steps, 2, 4, B, width), F32),
            pltpu.VMEM((steps, 2, 3, 4, B, width), F32),
            pltpu.VMEM((steps, 2, 3, B, width), F32),
            pltpu.VMEM((steps, rows + B, width), F32),
            pltpu.SemaphoreType.DMA((2,)),
            pltpu.SemaphoreType.DMA((copies,)),
            pltpu.SemaphoreType.DMA((copies,)),
        ]
        + [pltpu.VMEM((4, B, width), F32)] * steps
        + [pltpu.VMEM((2, 4, 4, 2, 3, H, width), BF16)] * (steps - 1)
        + [pltpu.VMEM((4, 2, H, width), BF16)] * (steps - 1),
        compiler_params=pltpu.CompilerParams(collective_id=0, has_side_effects=True, vmem_limit_bytes=67_043_328),
        name="window",
    )(
        dest, relative_map.transpose(1, 2, 0), pred, last, diag_row, parent, chain_map.transpose(0, 2, 1),
        src_panels.reshape(src, 2, B, width), targets[:, 0],
    )
    return out[:, None]


def solution(mesh):
    return jax.shard_map(
        local,
        mesh=mesh,
        in_specs=(
            P(None, "col", "row", None),
            P("col", "row", None),
            P("col"),
            P("col", None),
            P("col", None, "row"),
            P(),
            P(),
            P(None, None, "row"),
        ),
        out_specs=P(None, "col", "row", None),
        check_vma=False,
    )
```

time: 293 us -> 199 us (0.68)
  Pallas kernels: 287 us -> 193 us
  other arithmetic: 0 us -> 3.02 us
  local copies, waits for them, and re-layouts: 4.83 us -> 1.87 us
    pallas_call x13 -> x1, Pallas kernels: 287 us -> 193 us  [local(): pl.pallas_call(window_kernel, out_shape=jax.ShapeDtypeStruct((steps, rows...]
where the time goes in v4:
time: 199 us
  Pallas kernels  193 us (97%)
  other arithmetic  3.02 us (2%)
    pallas_call x1, Pallas kernels, local(): pl.pallas_call(window_kernel, out_shape=jax.ShapeDtypeStruct((steps, rows...  193 us

profile of v4, /device:TPU:1, one launch (start us, length us, event | category | flops | bytes accessed | tf_op | source)
XLA Modules:
  0.0 198.9 jit_solution(5667551715202185004)
XLA Ops:
  0.7 0.8 select_reduce_fusion.1
  1.5 0.6 compare_select_fusion.last_ref
  2.1 1.0 select_reduce_fusion
  3.1 0.6 compare_select_fusion.1.pred_ref
  3.7 193.4 %window.1 = f32[4,256,128]{2,1,0:T(8,128)} custom-call(s32[4,64]{1,0:T(4,128)} %bitcast.15, s32[4,2,64]{2,1,0:T(2,128)} %bitcast.16, s32[4,64]{1,0:T(4,128)} %compare_select_fusion.1.pred_ref, s32[4,32]{1,0:T(4,128)} %compare_select_fusion.last_ref, s32[4,32]{1,0:T(4,128)} %root_ref.1, s32[3,32]{1,0:T(4,128)} %parent_ref.1, s32[3,2,32]{2,1,0:T(2,128)} %bitcast.17, ...), custom_call_target="tpu_custom_call" | custom-call | tf_op jit(solution)/shard_map/window/pallas_call | solution.py:446
  197.1 1.9 copy.13
  (2 shorter events, 0.0 us)

commit v5 on v4

--- a/solution.py
+++ b/solution.py
@@ -11,6 +11,7 @@
 BF16 = jnp.bfloat16
 B = 128
 H = B // 2
+QUARTERS = (0, 1, 3, 2)
 TRANS_B = (((1,), (1,)), ((), ()))
 TRANS_A = (((0,), (0,)), ((), ()))
 MESH = pl.DeviceIdType.MESH
@@ -33,44 +34,40 @@
 
 
 def cholesky_inverse(a, midway=None):
-    n = a.shape[0]
-    lane = lax.broadcasted_iota(jnp.int32, (8, n), 1)
-    sub = lax.broadcasted_iota(jnp.int32, (8, n), 0)
+    n, nb = a.shape[0], 16
+    lane = lax.broadcasted_iota(jnp.int32, (nb, n), 1)
+    sub = lax.broadcasted_iota(jnp.int32, (nb, n), 0)
     upper, inverse = [], []
-    next_a, rest_a, next_w, rest_w = a[:8], a[8:], None, None
-    for j in range(n // 8):
-        if j == 10 and midway is not None:
+    next_a, next_w = a, None
+    for j in range(n // nb):
+        if j == 2 and midway is not None:
             midway()
-        pa = next_a
-        pw = (lane == sub + 8 * j).astype(F32)
+        pa, rest_a = next_a[:nb], next_a[nb:]
+        pw = (lane == sub + nb * j).astype(F32)
         if next_w is not None:
-            pw = pw + next_w
-        cols = [jnp.broadcast_to(pa[:, 8 * j + t : 8 * j + t + 1], (8, n)) for t in range(8)]
-        pivots = jnp.zeros((8, n), F32)
-        for t in range(8):
+            pw = pw + next_w[:nb]
+        cols = [jnp.broadcast_to(pa[:, nb * j + t : nb * j + t + 1], (nb, n)) for t in range(nb)]
+        pivots = jnp.zeros((nb, n), F32)
+        for t in range(nb):
             d = jnp.broadcast_to(cols[t][t : t + 1], (8, n))
-            pivots = jnp.where(sub == t, d, pivots)
-            if t < 7:
-                ratio = jnp.where(sub > t, cols[t] * (1.0 / d), 0.0)
-                for v in range(t + 1, 8):
+            pivots = jnp.where(sub == t, jnp.concatenate([d, d], axis=0), pivots)
+            if t < nb - 1:
+                r = 1.0 / d
+                ratio = jnp.where(sub > t, cols[t] * jnp.concatenate([r, r], axis=0), 0.0)
+                for v in range(t + 1, nb):
                     cols[v] = cols[v] - ratio * cols[v][t : t + 1]
                 pa = pa - ratio * pa[t : t + 1]
                 pw = pw - ratio * pw[t : t + 1]
         scale = lax.rsqrt(pivots)
         scale = scale * (1.5 - 0.5 * pivots * scale * scale)
-        pa = jnp.where(lane >= sub + 8 * j, pa * scale, 0.0)
+        pa = jnp.where(lane >= sub + nb * j, pa * scale, 0.0)
         pw = pw * scale
         upper.append(pa)
         inverse.append(pw)
-        if j + 1 < n // 8:
-            both = jnp.concatenate([pa, pw], axis=1)
-            first = split_product(pa[:, 8 * j + 8 : 8 * j + 16], both)
-            next_a = rest_a[:8] - first[:, :n]
-            next_w = -first[:, n:] if rest_w is None else rest_w[:8] - first[:, n:]
-            if j + 2 < n // 8:
-                step = split_product(pa[:, 8 * j + 16 :], both)
-                rest_a = rest_a[8:] - step[:, :n]
-                rest_w = -step[:, n:] if rest_w is None else rest_w[8:] - step[:, n:]
+        if j + 1 < n // nb:
+            step = split_product(pa[:, nb * j + nb :], jnp.concatenate([pa, pw], axis=1))
+            next_a = rest_a - step[:, :n]
+            next_w = -step[:, n:] if next_w is None else next_w[nb:] - step[:, n:]
     return jnp.concatenate(upper, axis=0).T, jnp.concatenate(inverse, axis=0)
 
 
@@ -130,23 +127,26 @@
 
 class Broadcast:
     def __init__(self, copies, mine, out):
+        self.copies, self.mine, self.out = copies, mine, out
+        self.up, self.down, self.on = [], [], []
+
+    def start(self, part):
         row = lax.axis_index("row")
-        self.copies, self.out = copies, out
-        self.low, self.high = pl.ds(0, 8), pl.ds(8, 8)
-        self.up = [copies.start(mine.at[part], out.at[row, part], at_z(1)) for part in (self.low, self.high)]
-        self.down = [copies.start(mine.at[part], out.at[row, part], at_z(3)) for part in (self.high, self.low)]
-
-    def relay(self):
+        blocks = pl.ds(part * 8, 8)
+        self.up.append(self.copies.start(self.mine.at[blocks], self.out.at[row, blocks], at_z(1)))
+        self.down.append(self.copies.start(self.mine.at[blocks], self.out.at[row, blocks], at_z(3)))
+
+    def relay(self, part):
         row = lax.axis_index("row")
-        self.up[0].wait_recv()
-        ref = self.out.at[lax.rem(row + 3, 4), self.low]
-        self.on = [self.copies.start(ref, ref, at_z(1))]
-        self.down[0].wait_recv()
-        ref = self.out.at[lax.rem(row + 1, 4), self.high]
+        self.up[part].wait_recv()
+        ref = self.out.at[lax.rem(row + 3, 4), pl.ds(part * 8, 4)]
+        self.on.append(self.copies.start(ref, ref, at_z(1)))
+        self.down[part].wait_recv()
+        ref = self.out.at[lax.rem(row + 1, 4), pl.ds(part * 8 + 4, 4)]
         self.on.append(self.copies.start(ref, ref, at_z(3)))
 
     def finish(self):
-        for copy in [self.up[1], self.down[1]] + self.on:
+        for copy in self.on:
             copy.wait_recv()
 
 
@@ -205,10 +205,12 @@
             ref = self.line(h, move(4 - d)[0], what)
             self.done.append(self.copies.start(ref, ref, partner()))
 
-    def close(self):
+    def close_rows(self):
         self.done = []
         for h in range(2):
             self.close_half(h, self.rows, self.turned[h])
+
+    def close_head(self):
         for h in range(2):
             self.close_half(h, self.head, self.turned_head[h])
 
@@ -225,29 +227,34 @@
     def begin(self, previous, sums, slot):
         p = position()[2]
         if previous is not None:
-            self.copies.sent([previous.first])
+            self.copies.sent(previous.first)
         self.own = lambda i: sums[slot(i * 2 + p)]
-
-        @pl.loop(0, 16)
-        def _(i):
-            self.away[i // 4, lax.rem(i, 4)] = sums[slot(i * 2 + 1 - p)]
-
-        self.first = self.copies.start(self.away, self.in0, partner())
+        self.first = []
+        for d in (2, 1, 3, 0):
+            to = at_x(d)[0]
+
+            @pl.loop(0, 4)
+            def _(i):
+                self.away[to, i] = sums[slot((to * 4 + i) * 2 + 1 - p)]
+
+            self.first.append(self.copies.start(self.away.at[to], self.in0.at[to], partner()))
 
     def pair(self, previous):
         if previous is not None:
             self.copies.sent(previous.second)
-        self.first.wait_recv()
         acc, in0 = self.acc, self.in0
-
-        @pl.loop(0, 16)
-        def _(i):
-            acc[i // 4, lax.rem(i, 4)] = self.own(i) + in0[i // 4, lax.rem(i, 4)]
-
         self.second = []
+        for d, first in zip((2, 1, 3, 0), self.first):
+            to, peer = at_x(d)
+            first.wait_recv()
+
+            @pl.loop(0, 4)
+            def _(i):
+                acc[to, i] = self.own(to * 4 + i) + in0[to, i]
+
+            if d:
+                self.second.append(self.copies.start(acc.at[to, :, :B], self.in1.at[0, d - 1], peer))
         for d in (2, 1, 3):
-            to, peer = at_x(d)
-            self.second.append(self.copies.start(acc.at[to, :, :B], self.in1.at[0, d - 1], peer))
             to, peer = at_y(d)
             self.second.append(self.copies.start(acc.at[:, to, B:], self.in1.at[1, d - 1], peer))
 
@@ -288,7 +295,7 @@
 
 def window_kernel(
     dest_ref, map_ref, pred_ref, last_ref, root_ref, parent_ref, chain_ref, panel_hbm, target_ref, out_ref,
-    panels, zb, chosen, heads, sums, away, acc, in0, part, in1, in2, upd, load_sem, send_sem, recv_sem, *bufs,
+    panels, zb0, zb1, chosen, heads, sums, away, acc, in0, part, in1, in2, upd, load_sem, send_sem, recv_sem, *bufs,
 ):
     steps = target_ref.shape[0]
     diags, child, headbuf = bufs[:steps], bufs[steps : 2 * steps - 1], bufs[2 * steps - 1 :]
@@ -298,51 +305,50 @@
     copies = Copies(send_sem, recv_sem)
     load = pltpu.make_async_copy(panel_hbm, panels, load_sem.at[0])
 
-    def quarter(q):
-        return panel_hbm.at[pl.ds(q * 16, 16), 0]
-
-    own = pltpu.make_async_copy(quarter(row), zb.at[row], load_sem.at[1])
-    own.start()
+    def quarter(q, part):
+        return panel_hbm.at[pl.ds(q * 16 + part * 8, 8), 0]
+
+    zb = (zb0, zb1)
+    own = [pltpu.make_async_copy(quarter(row, i), zb[i].at[row], load_sem.at[1 + i]) for i in range(2)]
+    for copy in own:
+        copy.start()
     sums[src] = jnp.zeros(sums.shape[1:], F32)
     greet([partner()] + [at_z(d) for d in (1, 2, 3)] + [f(d)[1] for f in (at_x, at_y) for d in (1, 2, 3)])
-    opened = [copies.start(quarter(lax.rem(row + d, 4)), zb.at[row], at_z(d)) for d in (2, 1, 3)]
+    opened = [[copies.start(quarter(lax.rem(row + d, 4), i), zb[i].at[row], at_z(d)) for d in (2, 1, 3)] for i in range(2)]
     load.start()
-    own.wait()
-    for copy in opened:
-        copy.wait_recv()
-
-    def choose(s):
-        @pl.loop(0, 16)
+
+    def choose(s, part):
+        @pl.loop(0, 8)
         def _(j):
-            chosen[s, j] = zb[root_ref[s, dest_ref[s, row * 16 + j]], j]
+            i = part * 8 + j
+            chosen[s, i] = zb[part][root_ref[s, dest_ref[s, row * 16 + i]], j]
 
     def keep(s):
         @pl.loop(0, 16)
         def _(j):
             heads[s, row, j] = chosen[s, j]
 
-    def products(s, quarters):
-        @pl.loop(quarters[0] * 4, quarters[1] * 4)
+    def products(s, place):
+        quarter = lax.rem(row + QUARTERS[place], 4)
+
+        @pl.loop(0, 4)
         def _(g):
             prods = []
             for u in range(4):
-                i = g * 4 + u
+                i = quarter * 16 + g * 4 + u
                 first = map_ref[s, 0, i]
                 block = jnp.concatenate([panels[i, first], panels[i, 1 - first]], axis=0)
                 prods.append(
-                    lax.dot_general(block, heads[s, i // 16, lax.rem(i, 16)], TRANS_B, preferred_element_type=F32)
+                    lax.dot_general(block, heads[s, quarter, g * 4 + u], TRANS_B, preferred_element_type=F32)
                 )
             for u in range(4):
-                i = g * 4 + u
-                sums[i] = prods[u] + sums[pred_ref[s, i]]
+                i = quarter * 16 + g * 4 + u
+                sums[place * 16 + g * 4 + u] = prods[u] + sums[pred_ref[s, i]]
 
     reduces = [
         Reduce(copies, acc, away, in0.at[s], part.at[s], in1.at[s], in2.at[s], diags[s]) for s in range(steps)
     ]
-    casts = {}
-
-    def cast(s):
-        casts[s] = Broadcast(copies, chosen.at[s], heads.at[s])
+    casts = [Broadcast(copies, chosen.at[s], heads.at[s]) for s in range(steps)]
 
     def begin(s):
         reduces[s].begin(reduces[s - 1] if s else None, sums, lambda c: last_ref[s, c])
@@ -382,49 +388,67 @@
         out_ref[s] = panel
         return panel.astype(BF16)
 
-    choose(0)
-    cast(0)
+    def both(action):
+        for part in range(2):
+            action(part)
+
+    for part in range(2):
+        own[part].wait()
+        for copy in opened[part]:
+            copy.wait_recv()
+        choose(0, part)
+        casts[0].start(part)
     keep(0)
     for s in range(1, steps):
-        choose(s)
+        for part in range(2):
+            choose(s, part)
         keep(s)
-    casts[0].relay()
-    cast(1)
     load.wait()
+    products(0, 0)
+    both(casts[0].relay)
+    both(casts[1].start)
+    products(0, 1)
+    products(0, 2)
     casts[0].finish()
-    products(0, (0, 4))
+    products(0, 3)
     begin(0)
-    casts[1].relay()
     reduces[0].pair(None)
+    both(casts[1].relay)
+    for place in range(3):
+        products(1, place)
     casts[1].finish()
-    products(1, (0, 4))
+    products(1, 3)
     begin(1)
+    both(casts[2].start)
     reduces[0].cross()
     reduces[1].pair(reduces[0])
     reduces[0].finish(target_ref.at[0], upd.at[0, : 2 * B])
-    cast(2)
-    low = factor(0, casts[2].relay)
+    both(casts[2].relay)
+    low = factor(0, None)
     for s in range(steps - 1):
         ahead = s + 2 if s + 2 < steps else None
         exchange = Exchange(copies, low, child[s], headbuf[s])
         exchange.begin()
+        exchange.pick(root_ref[s + 1, parent_ref[s, me]])
         reduces[s + 1].cross()
-        exchange.pick(root_ref[s + 1, parent_ref[s, me]])
         if ahead:
-            casts[ahead].finish()
-            products(ahead, (0, 2))
+            products(ahead, 0)
+            products(ahead, 1)
         exchange.turn()
         if ahead:
-            products(ahead, (2, 4))
+            products(ahead, 2)
+            casts[ahead].finish()
+            products(ahead, 3)
             begin(ahead)
         reduces[s + 1].finish(target_ref.at[s + 1], upd.at[s + 1, : 2 * B])
-        exchange.close()
         midway = None
         if s + 3 < steps:
-            cast(s + 3)
-            midway = casts[s + 3].relay
+            both(casts[s + 3].start)
+            midway = functools.partial(both, casts[s + 3].relay)
+        exchange.close_rows()
         if ahead:
             reduces[ahead].pair(reduces[ahead - 1])
+        exchange.close_head()
         exchange.finish()
         low = factor(s + 1, midway)
     copies.finish()
@@ -436,13 +460,16 @@
     cols = lax.axis_size("col")
     dest = dest_owner.T
     index = jnp.arange(src)
-    before = (dest[:, :, None] == dest[:, None, :]) & (index[None, :] < index[:, None])
-    pred = jnp.max(jnp.where(before, index, -1), axis=2)
+    ahead = (index // 16 - lax.axis_index("row")) % 4
+    rank = jnp.where(ahead < 2, ahead, 5 - ahead) * 16 + index % 16
+    alive = index < live_counts[0]
+    before = (dest[:, :, None] == dest[:, None, :]) & (rank[None, :] < rank[:, None]) & alive
+    pred = jnp.max(jnp.where(before, rank, -1), axis=2)
     pred = jnp.where(pred < 0, src, pred).astype(jnp.int32)
-    mine = (dest[:, None, :] == jnp.arange(cols)[:, None]) & (index < live_counts[0])
-    last = jnp.max(jnp.where(mine, index, -1), axis=2)
+    mine = (dest[:, None, :] == jnp.arange(cols)[:, None]) & alive
+    last = jnp.max(jnp.where(mine, rank, -1), axis=2)
     last = jnp.where(last < 0, src, last).astype(jnp.int32)
-    copies = 3 + steps * 22 + (steps - 1) * 43
+    copies = 6 + steps * 27 + (steps - 1) * 43
     out = pl.pallas_call(
         window_kernel,
         out_shape=jax.ShapeDtypeStruct((steps, rows, width), F32),
@@ -450,7 +477,8 @@
         out_specs=VMEM,
         scratch_shapes=[
             pltpu.VMEM((src, 2, B, width), BF16),
-            pltpu.VMEM((4, 16, B, width), BF16),
+            pltpu.VMEM((4, 8, B, width), BF16),
+            pltpu.VMEM((4, 8, B, width), BF16),
             pltpu.VMEM((steps, 16, B, width), BF16),
             pltpu.VMEM((steps, 4, 16, B, width), BF16),
             pltpu.VMEM((src + 1, rows, width), F32),
@@ -461,7 +489,7 @@
             pltpu.VMEM((steps, 2, 3, 4, B, width), F32),
             pltpu.VMEM((steps, 2, 3, B, width), F32),
             pltpu.VMEM((steps, rows + B, width), F32),
-            pltpu.SemaphoreType.DMA((2,)),
+            pltpu.SemaphoreType.DMA((3,)),
             pltpu.SemaphoreType.DMA((copies,)),
             pltpu.SemaphoreType.DMA((copies,)),
         ]

time: 199 us -> 188 us (0.945)
  Pallas kernels: 193 us -> 182 us
    pallas_call x1, Pallas kernels: 193 us -> 182 us  [local(): pl.pallas_call(window_kernel, out_shape=jax.ShapeDtypeStruct((steps, rows...]
where the time goes in v5:
time: 188 us; the launch traced here: 187 us
  Pallas kernels  182 us (97%)
  other arithmetic  3.1 us (2%)
    pallas_call x1, Pallas kernels, local(): pl.pallas_call(window_kernel, out_shape=jax.ShapeDtypeStruct((steps, rows...  182 us

profile of v5, /device:TPU:1, one launch (start us, length us, event | category | flops | bytes accessed | tf_op | source)
XLA Modules:
  0.0 187.5 jit_solution(2742578560965250208)
XLA Ops:
  0.7 0.8 select_reduce_fusion.1
  1.5 0.6 compare_select_fusion.last_ref
  2.1 0.1 broadcast_compare_fusion
  2.2 1.0 select_reduce_fusion
  3.2 0.6 compare_select_fusion.1.pred_ref
  3.8 181.8 %window.1 = f32[4,256,128]{2,1,0:T(8,128)} custom-call(s32[4,64]{1,0:T(4,128)} %bitcast.15, s32[4,2,64]{2,1,0:T(2,128)} %bitcast.16, s32[4,64]{1,0:T(4,128)} %compare_select_fusion.1.pred_ref, s32[4,32]{1,0:T(4,128)} %compare_select_fusion.last_ref, s32[4,32]{1,0:T(4,128)} %root_ref.1, s32[3,32]{1,0:T(4,128)} %parent_ref.1, s32[3,2,32]{2,1,0:T(2,128)} %bitcast.17, ...), custom_call_target="tpu_custom_call" | custom-call | tf_op jit(solution)/shard_map/window/pallas_call | solution.py:473
  185.6 1.9 copy.13
  (2 shorter events, 0.0 us)

commit v6 on v5

--- a/solution.py
+++ b/solution.py
@@ -33,15 +33,13 @@
     return lax.dot_general(lefts, rights, TRANS_A, preferred_element_type=F32)
 
 
-def cholesky_inverse(a, midway=None):
+def cholesky_inverse(a):
     n, nb = a.shape[0], 16
     lane = lax.broadcasted_iota(jnp.int32, (nb, n), 1)
     sub = lax.broadcasted_iota(jnp.int32, (nb, n), 0)
     upper, inverse = [], []
     next_a, next_w = a, None
     for j in range(n // nb):
-        if j == 2 and midway is not None:
-            midway()
         pa, rest_a = next_a[:nb], next_a[nb:]
         pw = (lane == sub + nb * j).astype(F32)
         if next_w is not None:
@@ -353,33 +351,29 @@
     def begin(s):
         reduces[s].begin(reduces[s - 1] if s else None, sums, lambda c: last_ref[s, c])
 
-    def factor(s, midway):
-        diag = reduces[s].diagonal(root_ref[s, me])
-        upd[s, 2 * B :] = diag
-        if s:
-
-            @pl.loop(0, 16)
-            def _(g):
-                lefts, rights = [], []
-                for u in range(2):
-                    k = g * 2 + u
-                    a, b, c = k // 8, lax.rem(k // 2, 4), u
-                    chosen_child = parent_ref[s - 1, k] == me
-                    head = jnp.concatenate([child[s - 1][h, a, b, c, 2] for h in range(2)], axis=0)
-                    head = jnp.where(chosen_child, head, jnp.zeros_like(head))
-                    first = chain_ref[s - 1, 0, k]
-                    left_out = root_ref[s - 1, k] == row
-                    blocks = []
-                    for q in (first, 1 - first):
-                        block = jnp.concatenate([child[s - 1][h, a, b, c, q] for h in range(2)], axis=0)
-                        blocks.append(jnp.where(left_out & (q == 0), jnp.zeros_like(block), block))
-                    lefts.append(jnp.concatenate(blocks + [head], axis=0))
-                    rights.append(head)
-                upd[s] -= lax.dot_general(
-                    jnp.concatenate(lefts, axis=1), jnp.concatenate(rights, axis=1), TRANS_B, preferred_element_type=F32
-                )
-
-        lower, inverse = cholesky_inverse(upd[s, 2 * B :], midway)
+    def children(s, parity):
+        @pl.loop(0, 8)
+        def _(g):
+            lefts, rights = [], []
+            for u in range(2):
+                a, b = g // 2, lax.rem(g, 2) * 2 + u
+                k = (a * 4 + b) * 2 + parity
+                mine = parent_ref[s - 1, k] == me
+                head = jnp.concatenate([child[s - 1][h, a, b, parity, 2] for h in range(2)], axis=0)
+                head = jnp.where(mine, head, jnp.zeros_like(head))
+                first = chain_ref[s - 1, 0, k]
+                left_out = root_ref[s - 1, k] == row
+                blocks = [jnp.concatenate([child[s - 1][h, a, b, parity, q] for h in range(2)], axis=0) for q in range(2)]
+                blocks[0] = jnp.where(left_out, jnp.zeros_like(blocks[0]), blocks[0])
+                blocks = [jnp.where(first == q, blocks[0], blocks[1]) for q in range(2)]
+                lefts.append(jnp.concatenate(blocks + [head], axis=0))
+                rights.append(head)
+            upd[s] -= lax.dot_general(
+                jnp.concatenate(lefts, axis=1), jnp.concatenate(rights, axis=1), TRANS_B, preferred_element_type=F32
+            )
+
+    def factor(s):
+        lower, inverse = cholesky_inverse(upd[s, 2 * B :])
         solved = lax.dot_general(
             upd[s, : 2 * B], inverse, TRANS_B, precision=lax.Precision.HIGHEST, preferred_element_type=F32
         )
@@ -414,22 +408,28 @@
     begin(0)
     reduces[0].pair(None)
     both(casts[1].relay)
+    casts[2].start(0)
     for place in range(3):
         products(1, place)
     casts[1].finish()
     products(1, 3)
     begin(1)
-    both(casts[2].start)
     reduces[0].cross()
     reduces[1].pair(reduces[0])
+    casts[2].relay(0)
     reduces[0].finish(target_ref.at[0], upd.at[0, : 2 * B])
-    both(casts[2].relay)
-    low = factor(0, None)
+    casts[2].start(1)
+    upd[0, 2 * B :] = reduces[0].diagonal(root_ref[0, me])
+    low = factor(0)
     for s in range(steps - 1):
         ahead = s + 2 if s + 2 < steps else None
         exchange = Exchange(copies, low, child[s], headbuf[s])
         exchange.begin()
         exchange.pick(root_ref[s + 1, parent_ref[s, me]])
+        if ahead:
+            casts[ahead].relay(1)
+        if s + 3 < steps:
+            casts[s + 3].start(0)
         reduces[s + 1].cross()
         if ahead:
             products(ahead, 0)
@@ -441,16 +441,18 @@
             products(ahead, 3)
             begin(ahead)
         reduces[s + 1].finish(target_ref.at[s + 1], upd.at[s + 1, : 2 * B])
-        midway = None
         if s + 3 < steps:
-            both(casts[s + 3].start)
-            midway = functools.partial(both, casts[s + 3].relay)
-        exchange.close_rows()
+            casts[s + 3].relay(0)
+            casts[s + 3].start(1)
         if ahead:
             reduces[ahead].pair(reduces[ahead - 1])
+        exchange.close_rows()
         exchange.close_head()
+        upd[s + 1, 2 * B :] = reduces[s + 1].diagonal(root_ref[s + 1, me])
+        children(s + 1, p)
         exchange.finish()
-        low = factor(s + 1, midway)
+        children(s + 1, 1 - p)
+        low = factor(s + 1)
     copies.finish()
 
 

time: 188 us -> 182 us (0.968)
  Pallas kernels: 182 us -> 176 us
    pallas_call x1, Pallas kernels: 182 us -> 176 us  [local(): pl.pallas_call(window_kernel, out_shape=jax.ShapeDtypeStruct((steps, rows...]
where the time goes in v6:
time: 182 us
  Pallas kernels  176 us (97%)
  other arithmetic  3.1 us (2%)
  local copies, waits for them, and re-layouts  1.87 us (1%)
    pallas_call x1, Pallas kernels, local(): pl.pallas_call(window_kernel, out_shape=jax.ShapeDtypeStruct((steps, rows...  176 us

profile of v6, /device:TPU:1, one launch (start us, length us, event | category | flops | bytes accessed | tf_op | source)
XLA Modules:
  0.0 181.6 jit_solution(16186966624412634864)
XLA Ops:
  0.7 0.8 select_reduce_fusion.1
  1.5 0.6 compare_select_fusion.last_ref
  2.1 0.1 broadcast_compare_fusion
  2.2 1.0 select_reduce_fusion
  3.2 0.6 compare_select_fusion.1.pred_ref
  3.8 175.9 %window.1 = f32[4,256,128]{2,1,0:T(8,128)} custom-call(s32[4,64]{1,0:T(4,128)} %bitcast.15, s32[4,2,64]{2,1,0:T(2,128)} %bitcast.16, s32[4,64]{1,0:T(4,128)} %compare_select_fusion.1.pred_ref, s32[4,32]{1,0:T(4,128)} %compare_select_fusion.last_ref, s32[4,32]{1,0:T(4,128)} %root_ref.1, s32[3,32]{1,0:T(4,128)} %parent_ref.1, s32[3,2,32]{2,1,0:T(2,128)} %bitcast.17, ...), custom_call_target="tpu_custom_call" | custom-call | tf_op jit(solution)/shard_map/window/pallas_call | solution.py:475
  179.7 1.9 %copy.13 = f32[4,1,256,128]{3,2,1,0:T(8,128)} copy(f32[4,1,256,128]{3,2,1,0:T(8,128)} %bitcast.11) | data formatting | bytes 1048576
  (2 shorter events, 0.0 us)

commit v7 on v6

--- a/solution.py
+++ b/solution.py
@@ -218,8 +218,8 @@
 
 
 class Reduce:
-    def __init__(self, copies, acc, away, in0, part, in1, in2, zbuf):
-        self.copies, self.acc, self.away = copies, acc, away
+    def __init__(self, copies, acc, away, in0, part, far, in1, in2, zbuf):
+        self.copies, self.acc, self.away, self.far = copies, acc, away, far
         self.in0, self.part, self.in1, self.in2, self.zbuf = in0, part, in1, in2, zbuf
 
     def begin(self, previous, sums, slot):
@@ -239,22 +239,36 @@
 
     def pair(self, previous):
         if previous is not None:
-            self.copies.sent(previous.second)
-        acc, in0 = self.acc, self.in0
-        self.second = []
+            self.copies.sent(previous.opened + previous.second)
+        acc, in0, far = self.acc, self.in0, self.far
+        self.opened = []
         for d, first in zip((2, 1, 3, 0), self.first):
-            to, peer = at_x(d)
+            to = at_x(d)[0]
             first.wait_recv()
 
             @pl.loop(0, 4)
             def _(i):
                 acc[to, i] = self.own(to * 4 + i) + in0[to, i]
 
-            if d:
-                self.second.append(self.copies.start(acc.at[to, :, :B], self.in1.at[0, d - 1], peer))
-        for d in (2, 1, 3):
-            to, peer = at_y(d)
-            self.second.append(self.copies.start(acc.at[:, to, B:], self.in1.at[1, d - 1], peer))
+            if d == 2:
+                self.opened.append(self.copies.start(acc.at[to, :2, :B], far.at[0, 0], at_x(1)[1]))
+                self.opened.append(self.copies.start(acc.at[to, 2:, :B], far.at[0, 1], at_x(3)[1]))
+        to = at_y(2)[0]
+        self.opened.append(self.copies.start(acc.at[:2, to, B:], far.at[1, 0], at_y(1)[1]))
+        self.opened.append(self.copies.start(acc.at[2:, to, B:], far.at[1, 1], at_y(3)[1]))
+
+    def combine(self):
+        for copy in self.opened:
+            copy.wait_recv()
+        acc, far, in1 = self.acc, self.far, self.in1
+        self.second = []
+        for n, d in enumerate((1, 3)):
+            (to_x, peer_x), (to_y, peer_y) = at_x(d), at_y(d)
+            for i in range(2):
+                acc[to_x, 2 * n + i, :B] += far[0, n, i]
+                acc[2 * n + i, to_y, B:] += far[1, n, i]
+            self.second.append(self.copies.start(acc.at[to_x, :, :B], in1.at[0, n], peer_x))
+            self.second.append(self.copies.start(acc.at[:, to_y, B:], in1.at[1, n], peer_y))
 
     def cross(self):
         x, y, _, _ = position()
@@ -264,8 +278,8 @@
 
         @pl.loop(0, 4)
         def _(i):
-            part[0, i] = acc[x, i, :B] + (in1[0, 0, i] + in1[0, 1, i] + in1[0, 2, i])
-            part[1, i] = acc[i, y, B:] + (in1[1, 0, i] + in1[1, 1, i] + in1[1, 2, i])
+            part[0, i] = acc[x, i, :B] + (in1[0, 0, i] + in1[0, 1, i])
+            part[1, i] = acc[i, y, B:] + (in1[1, 0, i] + in1[1, 1, i])
 
         self.third = []
         for d in (2, 1, 3):
@@ -293,7 +307,7 @@
 
 def window_kernel(
     dest_ref, map_ref, pred_ref, last_ref, root_ref, parent_ref, chain_ref, panel_hbm, target_ref, out_ref,
-    panels, zb0, zb1, chosen, heads, sums, away, acc, in0, part, in1, in2, upd, load_sem, send_sem, recv_sem, *bufs,
+    panels, zb0, zb1, chosen, heads, sums, away, acc, in0, part, far, in1, in2, upd, load_sem, send_sem, recv_sem, *bufs,
 ):
     steps = target_ref.shape[0]
     diags, child, headbuf = bufs[:steps], bufs[steps : 2 * steps - 1], bufs[2 * steps - 1 :]
@@ -344,7 +358,7 @@
                 sums[place * 16 + g * 4 + u] = prods[u] + sums[pred_ref[s, i]]
 
     reduces = [
-        Reduce(copies, acc, away, in0.at[s], part.at[s], in1.at[s], in2.at[s], diags[s]) for s in range(steps)
+        Reduce(copies, acc, away, in0.at[s], part.at[s], far.at[s], in1.at[s], in2.at[s], diags[s]) for s in range(steps)
     ]
     casts = [Broadcast(copies, chosen.at[s], heads.at[s]) for s in range(steps)]
 
@@ -407,7 +421,9 @@
     products(0, 3)
     begin(0)
     reduces[0].pair(None)
-    both(casts[1].relay)
+    casts[1].relay(0)
+    reduces[0].combine()
+    casts[1].relay(1)
     casts[2].start(0)
     for place in range(3):
         products(1, place)
@@ -419,6 +435,7 @@
     casts[2].relay(0)
     reduces[0].finish(target_ref.at[0], upd.at[0, : 2 * B])
     casts[2].start(1)
+    reduces[1].combine()
     upd[0, 2 * B :] = reduces[0].diagonal(root_ref[0, me])
     low = factor(0)
     for s in range(steps - 1):
@@ -449,6 +466,8 @@
         exchange.close_rows()
         exchange.close_head()
         upd[s + 1, 2 * B :] = reduces[s + 1].diagonal(root_ref[s + 1, me])
+        if ahead:
+            reduces[ahead].combine()
         children(s + 1, p)
         exchange.finish()
         children(s + 1, 1 - p)
@@ -471,7 +490,7 @@
     mine = (dest[:, None, :] == jnp.arange(cols)[:, None]) & alive
     last = jnp.max(jnp.where(mine, rank, -1), axis=2)
     last = jnp.where(last < 0, src, last).astype(jnp.int32)
-    copies = 6 + steps * 27 + (steps - 1) * 43
+    copies = 6 + steps * 29 + (steps - 1) * 43
     out = pl.pallas_call(
         window_kernel,
         out_shape=jax.ShapeDtypeStruct((steps, rows, width), F32),
@@ -488,7 +507,8 @@
             pltpu.VMEM((4, 4, rows, width), F32),
             pltpu.VMEM((steps, 4, 4, rows, width), F32),
             pltpu.VMEM((steps, 2, 4, B, width), F32),
-            pltpu.VMEM((steps, 2, 3, 4, B, width), F32),
+            pltpu.VMEM((steps, 2, 2, 2, B, width), F32),
+            pltpu.VMEM((steps, 2, 2, 4, B, width), F32),
             pltpu.VMEM((steps, 2, 3, B, width), F32),
             pltpu.VMEM((steps, rows + B, width), F32),
             pltpu.SemaphoreType.DMA((3,)),

time: 182 us -> 178 us (0.978)
  Pallas kernels: 176 us -> 172 us
    pallas_call x1, Pallas kernels: 176 us -> 172 us  [local(): pl.pallas_call(window_kernel, out_shape=jax.ShapeDtypeStruct((steps, rows...]
where the time goes in v7:
time: 178 us
  Pallas kernels  172 us (97%)
  other arithmetic  3.1 us (2%)
  local copies, waits for them, and re-layouts  1.87 us (1%)
    pallas_call x1, Pallas kernels, local(): pl.pallas_call(window_kernel, out_shape=jax.ShapeDtypeStruct((steps, rows...  172 us

profile of v7, /device:TPU:1, one launch (start us, length us, event | category | flops | bytes accessed | tf_op | source)
XLA Modules:
  0.0 177.6 jit_solution(8851551612633341755)
XLA Ops:
  0.7 0.8 select_reduce_fusion.1
  1.5 0.6 compare_select_fusion.last_ref
  2.1 0.1 broadcast_compare_fusion
  2.2 1.0 select_reduce_fusion
  3.2 0.6 compare_select_fusion.1.pred_ref
  3.8 172.0 %window.1 = f32[4,256,128]{2,1,0:T(8,128)} custom-call(s32[4,64]{1,0:T(4,128)} %bitcast.15, s32[4,2,64]{2,1,0:T(2,128)} %bitcast.16, s32[4,64]{1,0:T(4,128)} %compare_select_fusion.1.pred_ref, s32[4,32]{1,0:T(4,128)} %compare_select_fusion.last_ref, s32[4,32]{1,0:T(4,128)} %root_ref.1, s32[3,32]{1,0:T(4,128)} %parent_ref.1, s32[3,2,32]{2,1,0:T(2,128)} %bitcast.17, ...), custom_call_target="tpu_custom_call" | custom-call | tf_op jit(solution)/shard_map/window/pallas_call | solution.py:494
  175.8 1.9 %copy.13 = f32[4,1,256,128]{3,2,1,0:T(8,128)} copy(f32[4,1,256,128]{3,2,1,0:T(8,128)} %bitcast.11) | data formatting | bytes 1048576
  (2 shorter events, 0.0 us)

commit v8 on v7

--- a/solution.py
+++ b/solution.py
@@ -306,7 +306,8 @@
 
 
 def window_kernel(
-    dest_ref, map_ref, pred_ref, last_ref, root_ref, parent_ref, chain_ref, panel_hbm, target_ref, out_ref,
+    dest_hbm, map_hbm, pred_hbm, last_hbm, root_hbm, parent_hbm, chain_hbm, panel_hbm, target_hbm, out_ref,
+    dest_ref, map_ref, pred_ref, last_ref, root_ref, parent_ref, chain_ref, target_ref,
     panels, zb0, zb1, chosen, heads, sums, away, acc, in0, part, far, in1, in2, upd, load_sem, send_sem, recv_sem, *bufs,
 ):
     steps = target_ref.shape[0]
@@ -320,6 +321,15 @@
     def quarter(q, part):
         return panel_hbm.at[pl.ds(q * 16 + part * 8, 8), 0]
 
+    tables = [
+        pltpu.make_async_copy(a, b, load_sem.at[3 + n])
+        for n, (a, b) in enumerate(
+            (
+                (dest_hbm, dest_ref), (map_hbm, map_ref), (pred_hbm, pred_ref), (last_hbm, last_ref),
+                (root_hbm, root_ref), (parent_hbm, parent_ref), (chain_hbm, chain_ref), (target_hbm, target_ref),
+            )
+        )
+    ]
     zb = (zb0, zb1)
     own = [pltpu.make_async_copy(quarter(row, i), zb[i].at[row], load_sem.at[1 + i]) for i in range(2)]
     for copy in own:
@@ -327,7 +337,11 @@
     sums[src] = jnp.zeros(sums.shape[1:], F32)
     greet([partner()] + [at_z(d) for d in (1, 2, 3)] + [f(d)[1] for f in (at_x, at_y) for d in (1, 2, 3)])
     opened = [[copies.start(quarter(lax.rem(row + d, 4), i), zb[i].at[row], at_z(d)) for d in (2, 1, 3)] for i in range(2)]
+    for table in tables:
+        table.start()
     load.start()
+    for table in tables:
+        table.wait()
 
     def choose(s, part):
         @pl.loop(0, 8)
@@ -494,9 +508,17 @@
     out = pl.pallas_call(
         window_kernel,
         out_shape=jax.ShapeDtypeStruct((steps, rows, width), F32),
-        in_specs=[SMEM] * 7 + [ANY, VMEM],
+        in_specs=[ANY] * 9,
         out_specs=VMEM,
         scratch_shapes=[
+            pltpu.SMEM(dest.shape, jnp.int32),
+            pltpu.SMEM((steps, 2, src), jnp.int32),
+            pltpu.SMEM(pred.shape, jnp.int32),
+            pltpu.SMEM(last.shape, jnp.int32),
+            pltpu.SMEM(diag_row.shape, jnp.int32),
+            pltpu.SMEM(parent.shape, jnp.int32),
+            pltpu.SMEM((steps - 1, 2, cols), jnp.int32),
+            pltpu.VMEM((steps, rows, width), F32),
             pltpu.VMEM((src, 2, B, width), BF16),
             pltpu.VMEM((4, 8, B, width), BF16),
             pltpu.VMEM((4, 8, B, width), BF16),
@@ -511,7 +533,7 @@
             pltpu.VMEM((steps, 2, 2, 4, B, width), F32),
             pltpu.VMEM((steps, 2, 3, B, width), F32),
             pltpu.VMEM((steps, rows + B, width), F32),
-            pltpu.SemaphoreType.DMA((3,)),
+            pltpu.SemaphoreType.DMA((11,)),
             pltpu.SemaphoreType.DMA((copies,)),
             pltpu.SemaphoreType.DMA((copies,)),
         ]

time: 178 us -> 177 us (level)
  no operation moved by 1% of the time
where the time goes in v8:
time: 177 us
  Pallas kernels  171 us (97%)
  other arithmetic  3.1 us (2%)
  local copies, waits for them, and re-layouts  1.87 us (1%)
    pallas_call x1, Pallas kernels, local(): pl.pallas_call(window_kernel, out_shape=jax.ShapeDtypeStruct((steps, rows...  171 us

profile of v8, /device:TPU:1, one launch (start us, length us, event | category | flops | bytes accessed | tf_op | source)
XLA Modules:
  0.0 176.6 jit_solution(697510012401114632)
XLA Ops:
  0.7 0.8 select_reduce_fusion.1
  1.5 0.6 compare_select_fusion.last_hbm
  2.1 0.1 broadcast_compare_fusion
  2.2 1.0 select_reduce_fusion
  3.2 0.6 compare_select_fusion.1.pred_hbm
  3.8 171.0 %window.1 = f32[4,256,128]{2,1,0:T(8,128)} custom-call(s32[4,64]{1,0:T(4,128)} %bitcast.15, s32[4,2,64]{2,1,0:T(2,128)} %bitcast.16, s32[4,64]{1,0:T(4,128)} %compare_select_fusion.1.pred_hbm, s32[4,32]{1,0:T(4,128)} %compare_select_fusion.last_hbm, s32[4,32]{1,0:T(4,128)} %root_hbm.1, s32[3,32]{1,0:T(4,128)} %parent_hbm.1, s32[3,2,32]{2,1,0:T(2,128)} %bitcast.17, ...), custom_call_target="tpu_custom_call" | custom-call | tf_op jit(solution)/shard_map/window/pallas_call | solution.py:508
  174.8 1.9 %copy.13 = f32[4,1,256,128]{3,2,1,0:T(8,128)} copy(f32[4,1,256,128]{3,2,1,0:T(8,128)} %bitcast.11) | data formatting | bytes 1048576
  (2 shorter events, 0.0 us)

commit v9 on v8

--- a/solution.py
+++ b/solution.py
@@ -191,8 +191,10 @@
         ref = self.line(h, here, what)
         return [self.copies.start(ref, ref, move(d)[1]) for d in (2, 1, 3)], self.copies.start(ref, ref, partner())
 
-    def turn(self):
+    def turn_rows(self):
         self.turned = [self.turn_half(h, self.rows, self.opened[h]) for h in range(2)]
+
+    def turn_head(self):
         self.turned_head = [self.turn_half(h, self.head, self.opened_head[h]) for h in range(2)]
 
     def close_half(self, h, what, turned):
@@ -462,10 +464,11 @@
         if s + 3 < steps:
             casts[s + 3].start(0)
         reduces[s + 1].cross()
+        exchange.turn_rows()
         if ahead:
             products(ahead, 0)
             products(ahead, 1)
-        exchange.turn()
+        exchange.turn_head()
         if ahead:
             products(ahead, 2)
             casts[ahead].finish()

time: 177 us -> 177 us (level)
  no operation moved by 1% of the time
where the time goes in v9:
time: 177 us
  Pallas kernels  171 us (97%)
  other arithmetic  3.1 us (2%)
  local copies, waits for them, and re-layouts  1.87 us (1%)
    pallas_call x1, Pallas kernels, local(): pl.pallas_call(window_kernel, out_shape=jax.ShapeDtypeStruct((steps, rows...  171 us

profile of v9, /device:TPU:1, one launch (start us, length us, event | category | flops | bytes accessed | tf_op | source)
XLA Modules:
  0.0 177.0 jit_solution(18123213024457485146)
XLA Ops:
  0.7 0.8 select_reduce_fusion.1
  1.5 0.6 compare_select_fusion.last_hbm
  2.1 0.1 broadcast_compare_fusion
  2.2 1.0 select_reduce_fusion
  3.2 0.6 compare_select_fusion.1.pred_hbm
  3.8 171.4 %window.1 = f32[4,256,128]{2,1,0:T(8,128)} custom-call(s32[4,64]{1,0:T(4,128)} %bitcast.15, s32[4,2,64]{2,1,0:T(2,128)} %bitcast.16, s32[4,64]{1,0:T(4,128)} %compare_select_fusion.1.pred_hbm, s32[4,32]{1,0:T(4,128)} %compare_select_fusion.last_hbm, s32[4,32]{1,0:T(4,128)} %root_hbm.1, s32[3,32]{1,0:T(4,128)} %parent_hbm.1, s32[3,2,32]{2,1,0:T(2,128)} %bitcast.17, ...), custom_call_target="tpu_custom_call" | custom-call | tf_op jit(solution)/shard_map/window/pallas_call | solution.py:511
  175.2 1.9 %copy.13 = f32[4,1,256,128]{3,2,1,0:T(8,128)} copy(f32[4,1,256,128]{3,2,1,0:T(8,128)} %bitcast.11) | data formatting | bytes 1048576
  (2 shorter events, 0.0 us)
